TPU v7x, 32 devices: a whole 2x2x4 slice. The times are simulated.
32 devices in a mesh: seq: 8 (over y, x, core), head: 4 (over z).
Axes of the slice: x: 2, y: 2, z: 4, core: 2. Of those that a mesh axis runs over, the one named last changes fastest.
Arguments:
- frames: bfloat16 [8192, 1024], P(('seq', 'head')), may hold values from -6 to 6
- cotangent: bfloat16 [8192, 1024], P(('seq', 'head')), may hold values from -6 to 6
- norm_gain: float32 [1024], replicated, may hold values from 0.25 to 1.75
- w_qkv: bfloat16 [3, 1024, 1024], replicated
- w_out: bfloat16 [1024, 1024], replicated, may hold values from -0.1875 to 0.1875
Outputs:
- output: bfloat16 [8192, 1024], P(('seq', 'head'))
- grad_frames: bfloat16 [8192, 1024], P(('seq', 'head'))
- grad_qkv: float32 [3, 1024, 1024], P(None, 'seq', 'head')
- grad_out: float32 [1024, 1024], P('seq', 'head')
All inputs are finite; a program needn't handle non-finite values.
Results may differ from a plain program's by a relative error of at most 0.015.
Values may be sent and summed in bfloat16 or wider, within the bound.
A program may use at most 128 MiB of HBM per device.

v0:
```python
import functools

import jax
import jax.numpy as jnp
from jax import lax
from jax.experimental import pallas as pl
from jax.experimental.pallas import tpu as pltpu
from jax.sharding import PartitionSpec as P

HEAD_SIZE = 128
WINDOW = 128

EPSILON = 1e-05
MASKED = -1e30
AXES = ("seq", "head")


def dot(a, b, contract):
    return lax.dot_general(a, b, (contract, ((), ())), preferred_element_type=jnp.float32)


def bits_of(size):
    return list(range(size.bit_length() - 1))


def block_kernel(
    sizes, orders,
    frames, cotangent, gain, w_qkv_hbm, w_out_hbm,
    output, grad_frames, grad_qkv, grad_out,
    w_qkv, w_out, normed, normed_t, query, key, value, upstream, attended, attended_t,
    grad_query, grad_pair, shares, edge_out, edge_in, grad_normed, held, landed, halo,
    weight_sem, halo_send, halo_recv, edge_send, edge_recv, send_sem, recv_sem,
):
    seq_size, head_size = sizes
    devices = tiles = seq_size * head_size
    length, channels = frames.shape
    chunks, stages = len(orders), len(orders[0])
    tile_rows, tile_cols = held.shape[2:]
    place = {axis: lax.axis_index(axis) for axis in AXES}
    position = place["seq"] * head_size + place["head"]
    bf16, f32 = jnp.bfloat16, jnp.float32
    strip = min(256, channels)

    def neighbour(step):
        there = (position + step + devices) % devices
        return (there // head_size, there % head_size)

    def bit_at(order):
        axis, bit = order
        return (place[axis] // 2**bit) % 2

    def partner(order):
        axis, bit = order
        moved = place[axis] + (1 - 2 * bit_at(order)) * 2**bit
        return tuple(moved if name == axis else place[name] for name in AXES)

    weights = [pltpu.make_async_copy(w_out_hbm, w_out, weight_sem.at[3])]
    for which in range(3):
        weights.append(
            pltpu.make_async_copy(w_qkv_hbm.at[which], w_qkv.at[which], weight_sem.at[which])
        )
    for one in weights:
        one.start()

    greeted = [partner(order) for order in orders[0]] + [neighbour(1), neighbour(-1)]
    barrier = pltpu.get_barrier_semaphore()
    for device in greeted:
        pl.semaphore_signal(barrier, inc=1, device_id=device, device_id_type=pl.DeviceIdType.MESH)
    pl.semaphore_wait(barrier, len(greeted))

    def halo_copy(side):
        rows = pl.ds(length - WINDOW, WINDOW) if side == 0 else pl.ds(0, WINDOW)
        return pltpu.make_async_remote_copy(
            src_ref=frames.at[rows],
            dst_ref=halo.at[side],
            send_sem=halo_send.at[side],
            recv_sem=halo_recv.at[side],
            device_id=neighbour(1 if side == 0 else -1),
            device_id_type=pl.DeviceIdType.MESH,
        )

    halo_copy(0).start()
    halo_copy(1).start()

    def standardise(values):
        average = jnp.mean(values, axis=-1, keepdims=True)
        centered = values - average
        variance = jnp.mean(centered * centered, axis=-1, keepdims=True)
        inverse = lax.rsqrt(variance + EPSILON)
        return centered * inverse, inverse

    few = 64

    def norm_rows(source, target_row, rows):
        def one(step, carry):
            values = source[pl.ds(pl.multiple_of(step * few, few), few), :].astype(f32)
            rounded = (standardise(values)[0] * gain[...]).astype(bf16)
            normed[pl.ds(pl.multiple_of(target_row + step * few, few), few), :] = rounded
            return carry

        lax.fori_loop(0, rows // few, one, 0)

    def multiply_into(target, rows, left, weight, side):
        for start in range(0, channels, strip):
            cols = slice(start, start + strip)
            other = weight[:, cols] if side == 0 else weight[cols, :]
            target[rows, cols] = dot(left, other, ((1,), (side,))).astype(target.dtype)

    norm_rows(frames, WINDOW, length)
    own = slice(WINDOW, WINDOW + length)

    def turn(first, last):
        for start in range(first, last, 128):
            for col in range(0, channels, 128):
                tile = normed[start : start + 128, col : col + 128]
                normed_t[col : col + 128, start : start + 128] = tile.astype(f32).T.astype(bf16)

    turn(WINDOW, WINDOW + length)
    weights[0].wait()
    everything = slice(0, length)
    multiply_into(upstream, everything, cotangent[...], w_out, 1)
    for which, target, rows in ((0, query, everything), (1, key, own), (2, value, own)):
        weights[1 + which].wait()
        multiply_into(target, rows, normed[own, :], w_qkv.at[which], 0)
    for side in range(2):
        halo_copy(side).wait()
        start = side * (length + WINDOW)
        norm_rows(halo.at[side], start, WINDOW)
    for side in range(2):
        start = side * (length + WINDOW)
        rows = slice(start, start + WINDOW)
        multiply_into(key, rows, normed[rows, :], w_qkv.at[1], 0)
        multiply_into(value, rows, normed[rows, :], w_qkv.at[2], 0)

    wide = 2 * HEAD_SIZE
    pairs = channels // wide

    def edge_copy(side):
        return pltpu.make_async_remote_copy(
            src_ref=edge_out.at[side],
            dst_ref=edge_in.at[side],
            send_sem=edge_send.at[side],
            recv_sem=edge_recv.at[side],
            device_id=neighbour(-1 if side == 0 else 1),
            device_id_type=pl.DeviceIdType.MESH,
        )

    blocks = length // WINDOW
    span = 3 * WINDOW
    score_scale = HEAD_SIZE ** (-0.5)
    row = lax.broadcasted_iota(jnp.int32, (WINDOW, span), 0)
    col = lax.broadcasted_iota(jnp.int32, (WINDOW, span), 1)
    near = (col >= row) & (col <= row + 2 * WINDOW)

    def forward(pair, carry):
        for head in range(wide // HEAD_SIZE):
            lane = pl.multiple_of(pair * wide + head * HEAD_SIZE, HEAD_SIZE)
            lanes = pl.ds(lane, HEAD_SIZE)
            for block in range(blocks):
                rows = slice(block * WINDOW, (block + 1) * WINDOW)
                keys = slice(block * WINDOW, block * WINDOW + span)
                q, k, v = query[rows, lanes], key[keys, lanes], value[keys, lanes]
                frame = position * length + (block - 1) * WINDOW + col
                allowed = near & (frame >= 0) & (frame < devices * length)
                scores = jnp.where(allowed, dot(q, k, ((1,), (1,))) * score_scale, MASKED)
                share = jnp.exp(scores - jnp.max(scores, axis=-1, keepdims=True))
                share = (share * (1.0 / jnp.sum(share, axis=-1, keepdims=True))).astype(bf16)
                shares[pair * (wide // HEAD_SIZE) + head, block] = share
                mixed = dot(share, v, ((1,), (0,)))
                attended[rows, lanes] = mixed.astype(bf16)
                attended_t[lanes, rows] = mixed.T.astype(bf16)
        return carry

    def backward(pair, carry):
        for head in range(wide // HEAD_SIZE):
            lane = pl.multiple_of(pair * wide + head * HEAD_SIZE, HEAD_SIZE)
            lanes = pl.ds(lane, HEAD_SIZE)
            key_grads = [None] * (blocks + 2)
            value_grads = [None] * (blocks + 2)
            for block in range(blocks):
                rows = slice(block * WINDOW, (block + 1) * WINDOW)
                keys = slice(block * WINDOW, block * WINDOW + span)
                q, k, v, up = query[rows, lanes], key[keys, lanes], value[keys, lanes], upstream[rows, lanes]
                rounded = shares[pair * (wide // HEAD_SIZE) + head, block]
                share = rounded.astype(f32)
                grad = dot(up, v, ((1,), (1,)))
                centre = jnp.sum(share * grad, axis=-1, keepdims=True)
                grad = (share * (grad - centre) * score_scale).astype(bf16)
                grad_query[rows, lanes] = dot(grad, k, ((1,), (0,))).astype(bf16)
                key_grad = dot(grad, q, ((0,), (0,)))
                value_grad = dot(rounded, up, ((0,), (0,)))
                for part in range(3):
                    piece = slice(part * WINDOW, (part + 1) * WINDOW)
                    for sums, term in ((key_grads, key_grad[piece]), (value_grads, value_grad[piece])):
                        before = sums[block + part]
                        sums[block + part] = term if before is None else before + term
            for which, sums in enumerate((key_grads, value_grads)):
                for block in range(blocks + 2):
                    rows = slice(block * WINDOW, (block + 1) * WINDOW)
                    grad_pair[which, rows, lanes] = sums[block].astype(bf16)
        return carry

    def base(chunk, stage):
        total = 0
        for step in range(stage):
            total = total + bit_at(orders[chunk][step]) * (tiles >> (step + 1))
        return total

    def landing(stage):
        return tiles - (tiles >> stage)

    def copy(chunk, stage):
        half = tiles >> (stage + 1)
        order = orders[chunk][stage]
        other = base(chunk, stage) + (1 - bit_at(order)) * half
        return pltpu.make_async_remote_copy(
            src_ref=held.at[chunk, pl.ds(other, half)],
            dst_ref=landed.at[chunk, pl.ds(landing(stage), half)],
            send_sem=send_sem.at[chunk, stage],
            recv_sem=recv_sem.at[chunk, stage],
            device_id=partner(order),
            device_id_type=pl.DeviceIdType.MESH,
        )

    def advance(chunk, stage):
        copy(chunk, stage).wait()
        half = tiles >> (stage + 1)
        keep = base(chunk, stage + 1)
        if stage == stages - 1:
            total = held[chunk, keep].astype(f32) + landed[chunk, landing(stage)].astype(f32)
            if chunk == 0:
                grad_out[...] = total
            else:
                grad_qkv[chunk - 1] = total
            return

        def add(step, carry):
            total = held[chunk, keep + step].astype(f32) + landed[chunk, landing(stage) + step].astype(f32)
            held[chunk, keep + step] = total.astype(bf16)
            return carry

        lax.fori_loop(0, half, add, 0)
        copy(chunk, stage + 1).start()

    def tile_place(chunk, axis, index):
        total = 0
        for step, (name, bit) in enumerate(orders[chunk]):
            if name == axis:
                total = total + ((index // 2**bit) % 2) * (tiles >> (step + 1))
        return total

    def products(chunk, left, right, depth, half):
        def one(step, carry):
            block = 2 * step + half
            rows = pl.ds(pl.multiple_of(block * tile_rows, tile_rows), tile_rows)
            product = dot(left[rows, depth], right[...], ((1,), (0,))).astype(bf16)
            down = tile_place(chunk, "seq", block)
            for col in range(head_size):
                held[chunk, down + tile_place(chunk, "head", col)] = product[
                    :, col * tile_cols : (col + 1) * tile_cols
                ]
            return carry

        lax.fori_loop(0, seq_size // 2, one, 0)

    def launch(chunk, left, right, depth):
        mine = bit_at(orders[chunk][0])
        products(chunk, left, right, depth, 1 - mine)
        copy(chunk, 0).start()
        products(chunk, left, right, depth, mine)

    lax.fori_loop(0, pairs, forward, 0)
    launch(0, attended_t, cotangent, everything)
    lax.fori_loop(0, pairs // 2, backward, 0)
    advance(0, 0)
    lax.fori_loop(pairs // 2, pairs, backward, 0)
    launch(1, normed_t, grad_query, own)
    turn(0, WINDOW)
    turn(WINDOW + length, 2 * WINDOW + length)
    launch(2, normed_t, grad_pair.at[0], slice(0, 2 * WINDOW + length))
    advance(1, 0)
    launch(3, normed_t, grad_pair.at[1], slice(0, 2 * WINDOW + length))
    advance(2, 0)

    def pair_back(rows, cols):
        term = dot(grad_pair[0, rows, :], w_qkv[1, cols, :], ((1,), (1,)))
        return term + dot(grad_pair[1, rows, :], w_qkv[2, cols, :], ((1,), (1,)))

    for side in range(2):
        start = side * (length + WINDOW)
        for strip_start in range(0, channels, strip):
            cols = slice(strip_start, strip_start + strip)
            edge_out[side, :, cols] = pair_back(slice(start, start + WINDOW), cols).astype(bf16)
        edge_copy(side).start()
    advance(3, 0)
    for start in range(0, channels, strip):
        cols = slice(start, start + strip)
        mixed = dot(attended[...], w_out[:, cols], ((1,), (0,)))
        output[:, cols] = (frames[:, cols].astype(f32) + mixed).astype(bf16)
    advance(0, 1)
    for start in range(0, channels, strip):
        cols = slice(start, start + strip)
        grad_normed[:, cols] = pair_back(own, cols) + dot(grad_query[...], w_qkv[0, cols, :], ((1,), (1,)))
    advance(1, 1)
    advance(2, 1)
    advance(3, 1)

    def norm_back(step, carry):
        rows = pl.ds(pl.multiple_of(step * few, few), few)
        unit, inverse = standardise(frames[rows, :].astype(f32))
        grad = grad_normed[rows, :].astype(bf16).astype(f32) * gain[...]
        average = jnp.mean(grad, axis=-1, keepdims=True)
        along = jnp.mean(grad * unit, axis=-1, keepdims=True)
        grad = inverse * (grad - average - unit * along)
        grad_frames[rows, :] = (cotangent[rows, :].astype(f32) + grad).astype(bf16)
        return carry

    for stage in range(2, stages):
        for chunk in range(chunks):
            advance(chunk, stage)
        if stage == 2:
            edge_copy(0).wait()
            edge_copy(1).wait()
            grad_normed[:WINDOW, :] += edge_in[1].astype(f32)
            grad_normed[length - WINDOW :, :] += edge_in[0].astype(f32)
            lax.fori_loop(0, length // few, norm_back, 0)


def deliver_kernel(scale, output, grad_frames, grad_qkv, grad_out, *targets):
    targets[0][...] = output[...]
    targets[1][...] = grad_frames[...]
    targets[2][...] = grad_qkv[...] * scale
    targets[3][...] = grad_out[...] * scale


def shards(frames, cotangent, norm_gain, w_qkv, w_out):
    length, channels = frames.shape
    seq_size, head_size = lax.axis_size("seq"), lax.axis_size("head")
    devices = seq_size * head_size
    bordered = length + 2 * WINDOW
    tile_rows, tile_cols = channels // seq_size, channels // head_size
    outer = [("seq", bit) for bit in bits_of(seq_size)[1:]]
    along = [("head", bit) for bit in bits_of(head_size)]
    first = [("seq", 0)]
    orders = [
        first + outer + along,
        first + outer[::-1] + along,
        first + along[:1] + outer[::-1] + along[1:],
        first + outer[:1] + along[:1] + outer[1:] + along[1:],
    ]
    chunks, stages = len(orders), len(orders[0])
    bf16, f32 = jnp.bfloat16, jnp.float32
    vmem, anywhere = pl.BlockSpec(memory_space=pltpu.VMEM), pl.BlockSpec(memory_space=pl.ANY)
    dma = pltpu.SemaphoreType.DMA
    shapes = [
        jax.ShapeDtypeStruct((length, channels), bf16),
        jax.ShapeDtypeStruct((length, channels), bf16),
        jax.ShapeDtypeStruct((3, tile_rows, tile_cols), f32),
        jax.ShapeDtypeStruct((tile_rows, tile_cols), f32),
    ]
    results = pl.pallas_call(
        functools.partial(block_kernel, (seq_size, head_size), orders),
        out_shape=shapes,
        in_specs=[vmem, vmem, vmem, anywhere, anywhere],
        out_specs=[vmem] * 4,
        scratch_shapes=[
            pltpu.VMEM((3, channels, channels), bf16),
            pltpu.VMEM((channels, channels), bf16),
            pltpu.VMEM((bordered, channels), bf16),
            pltpu.VMEM((channels, bordered), bf16),
            pltpu.VMEM((length, channels), bf16),
            pltpu.VMEM((bordered, channels), bf16),
            pltpu.VMEM((bordered, channels), bf16),
            pltpu.VMEM((length, channels), bf16),
            pltpu.VMEM((length, channels), bf16),
            pltpu.VMEM((channels, length), bf16),
            pltpu.VMEM((length, channels), bf16),
            pltpu.VMEM((2, bordered, channels), bf16),
            pltpu.VMEM((channels // HEAD_SIZE, length // WINDOW, WINDOW, 3 * WINDOW), bf16),
            pltpu.VMEM((2, WINDOW, channels), bf16),
            pltpu.VMEM((2, WINDOW, channels), bf16),
            pltpu.VMEM((length, channels), f32),
            pltpu.VMEM((chunks, devices, tile_rows, tile_cols), bf16),
            pltpu.VMEM((chunks, devices, tile_rows, tile_cols), bf16),
            pltpu.VMEM((2, WINDOW, channels), bf16),
            dma((4,)),
            dma((2,)),
            dma((2,)),
            dma((2,)),
            dma((2,)),
            dma((chunks, stages)),
            dma((chunks, stages)),
        ],
        compiler_params=pltpu.CompilerParams(
            collective_id=0, has_side_effects=True, vmem_limit_bytes=60 * 2**20
        ),
        name="block",
    )(frames, cotangent, norm_gain.reshape(1, channels), w_qkv, w_out)
    return tuple(
        pl.pallas_call(
            functools.partial(deliver_kernel, (devices * length) ** (-0.5)),
            out_shape=shapes,
            in_specs=[vmem] * 4,
            out_specs=[vmem] * 4,
            name="deliver",
        )(*results)
    )


def solution(mesh):
    in_specs = (P(("seq", "head"), None), P(("seq", "head"), None), P(), P(), P())
    out_specs = (
        P(("seq", "head"), None),
        P(("seq", "head"), None),
        P(None, "seq", "head"),
        P("seq", "head"),
    )
    return jax.shard_map(shards, mesh=mesh, in_specs=in_specs, out_specs=out_specs, check_vma=False)
```

profile of v0, /device:TPU:0, one launch (start us, length us, event | category | flops | bytes accessed | tf_op | source)
XLA Modules:
  0.0 95.7 jit_solution(1568042298133144690)
XLA Ops:
  0.6 92.6 %block.1 = (bf16[256,1024]{1,0:T(8,128)(2,1)}, bf16[256,1024]{1,0:T(8,128)(2,1)}, f32[3,128,256]{2,1,0:T(8,128)}, f32[128,256]{1,0:T(8,128)}) custom-call(bf16[256,1024]{1,0:T(8,128)(2,1)} %frames.1, bf16[256,1024]{1,0:T(8,128)(2,1)} %cotangent.1, f32[1,1024]{1,0:T(1,128)} %bitcast.1, bf16[3,1024,1024]{2,1,0:T(8,128)(2,1)} %w_qkv_hbm.1, ...), custom_call_target="tpu_custom_call" | custom-call | tf_op jit(solution)/shard_map/block/pallas_call | solution.py:361
  93.2 2.5 %deliver.1 = (bf16[256,1024]{1,0:T(8,128)(2,1)}, bf16[256,1024]{1,0:T(8,128)(2,1)}, f32[3,128,256]{2,1,0:T(8,128)}, f32[128,256]{1,0:T(8,128)}) custom-call(bf16[256,1024]{1,0:T(8,128)(2,1)} %get-tuple-element.8.output, bf16[256,1024]{1,0:T(8,128)(2,1)} %get-tuple-element.9.grad_frames, f32[3,128,256]{2,1,0:T(8,128)} %get-tuple-element.10.grad_qkv, ...), custom_call_target="tpu_custom_call" | custom-call | tf_op jit(solution)/shard_map/deliver/pallas_call | solution.py:400
where the time goes:
time: 95.9 us; the launch traced here: 95.7 us
  Pallas kernels  95.1 us (99%)
    pallas_call x1, Pallas kernels, shards(): pl.pallas_call(functools.partial(block_kernel, (seq_size, head_size), ord...  92.6 us
    pallas_call x1, Pallas kernels, shards(): pl.pallas_call(functools.partial(deliver_kernel, (devices * length) ** (-...  2.51 us

commit v1 on v0

--- a/solution.py
+++ b/solution.py
@@ -24,20 +24,25 @@
 
 
 def block_kernel(
-    sizes, orders,
+    sizes,
     frames, cotangent, gain, w_qkv_hbm, w_out_hbm,
     output, grad_frames, grad_qkv, grad_out,
     w_qkv, w_out, normed, normed_t, query, key, value, upstream, attended, attended_t,
-    grad_query, grad_pair, shares, edge_out, edge_in, grad_normed, held, landed, halo,
-    weight_sem, halo_send, halo_recv, edge_send, edge_recv, send_sem, recv_sem,
+    grad_query, grad_pair, shares, edge_out, edge_in, grad_normed, halo, mail, got, held, landed, last,
+    weight_sem, halo_send, halo_recv, edge_send, edge_recv,
+    core_send, core_recv, stage_send, stage_recv, last_send, last_recv,
 ):
     seq_size, head_size = sizes
-    devices = tiles = seq_size * head_size
+    devices = seq_size * head_size
     length, channels = frames.shape
-    chunks, stages = len(orders), len(orders[0])
-    tile_rows, tile_cols = held.shape[2:]
-    place = {axis: lax.axis_index(axis) for axis in AXES}
-    position = place["seq"] * head_size + place["head"]
+    outer, part_rows, tile_cols = held.shape[2], held.shape[4], held.shape[5]
+    tile_rows = 2 * part_rows
+    bits = bits_of(outer)
+    orders = (bits, bits[::-1])
+    levels = len(bits)
+    seq, head = lax.axis_index("seq"), lax.axis_index("head")
+    core, row_block = seq % 2, seq // 2
+    position = seq * head_size + head
     bf16, f32 = jnp.bfloat16, jnp.float32
     strip = min(256, channels)
 
@@ -45,14 +50,14 @@
         there = (position + step + devices) % devices
         return (there // head_size, there % head_size)
 
-    def bit_at(order):
-        axis, bit = order
-        return (place[axis] // 2**bit) % 2
-
-    def partner(order):
-        axis, bit = order
-        moved = place[axis] + (1 - 2 * bit_at(order)) * 2**bit
-        return tuple(moved if name == axis else place[name] for name in AXES)
+    def bit_at(bit):
+        return (row_block // 2**bit) % 2
+
+    def partner(bit):
+        return (2 * (row_block + (1 - 2 * bit_at(bit)) * 2**bit) + core, head)
+
+    def along(step):
+        return (seq, (head + step) % head_size)
 
     weights = [pltpu.make_async_copy(w_out_hbm, w_out, weight_sem.at[3])]
     for which in range(3):
@@ -62,7 +67,9 @@
     for one in weights:
         one.start()
 
-    greeted = [partner(order) for order in orders[0]] + [neighbour(1), neighbour(-1)]
+    other_core = (2 * row_block + 1 - core, head)
+    greeted = [other_core] + [partner(bit) for bit in bits]
+    greeted += [along(step) for step in range(1, head_size)] + [neighbour(1), neighbour(-1)]
     barrier = pltpu.get_barrier_semaphore()
     for device in greeted:
         pl.semaphore_signal(barrier, inc=1, device_id=device, device_id_type=pl.DeviceIdType.MESH)
@@ -109,11 +116,19 @@
     norm_rows(frames, WINDOW, length)
     own = slice(WINDOW, WINDOW + length)
 
+    piece = min(128, tile_rows)
+
+    def store_turned(target, first, cols, turned):
+        for start in range(0, 128, piece):
+            block = (first + start) // tile_rows
+            down = (block // 2) * tile_rows + (first + start) % tile_rows
+            target[block % 2, pl.ds(pl.multiple_of(down, piece), piece), cols] = turned[start : start + piece]
+
     def turn(first, last):
         for start in range(first, last, 128):
             for col in range(0, channels, 128):
                 tile = normed[start : start + 128, col : col + 128]
-                normed_t[col : col + 128, start : start + 128] = tile.astype(f32).T.astype(bf16)
+                store_turned(normed_t, col, slice(start, start + 128), tile.astype(f32).T.astype(bf16))
 
     turn(WINDOW, WINDOW + length)
     weights[0].wait()
@@ -168,7 +183,7 @@
                 shares[pair * (wide // HEAD_SIZE) + head, block] = share
                 mixed = dot(share, v, ((1,), (0,)))
                 attended[rows, lanes] = mixed.astype(bf16)
-                attended_t[lanes, rows] = mixed.T.astype(bf16)
+                store_turned(attended_t, lane, rows, mixed.T.astype(bf16))
         return carry
 
     def backward(pair, carry):
@@ -200,130 +215,173 @@
                     grad_pair[which, rows, lanes] = sums[block].astype(bf16)
         return carry
 
-    def base(chunk, stage):
+    def spot(lane, block):
+        return sum(((block >> bit) & 1) * (outer >> (step + 1)) for step, bit in enumerate(orders[lane]))
+
+    def base(lane, stage):
         total = 0
         for step in range(stage):
-            total = total + bit_at(orders[chunk][step]) * (tiles >> (step + 1))
+            total = total + bit_at(orders[lane][step]) * (outer >> (step + 1))
         return total
 
     def landing(stage):
-        return tiles - (tiles >> stage)
-
-    def copy(chunk, stage):
-        half = tiles >> (stage + 1)
-        order = orders[chunk][stage]
-        other = base(chunk, stage) + (1 - bit_at(order)) * half
+        return outer - (outer >> stage)
+
+    def leaving(lane, stage):
+        return base(lane, stage) + (1 - bit_at(orders[lane][stage])) * (outer >> (stage + 1))
+
+    def core_copy(chunk):
         return pltpu.make_async_remote_copy(
-            src_ref=held.at[chunk, pl.ds(other, half)],
-            dst_ref=landed.at[chunk, pl.ds(landing(stage), half)],
-            send_sem=send_sem.at[chunk, stage],
-            recv_sem=recv_sem.at[chunk, stage],
-            device_id=partner(order),
+            src_ref=mail.at[chunk],
+            dst_ref=got.at[chunk],
+            send_sem=core_send.at[chunk],
+            recv_sem=core_recv.at[chunk],
+            device_id=other_core,
             device_id_type=pl.DeviceIdType.MESH,
         )
 
+    def stage_copy(chunk, lane, stage):
+        half = outer >> (stage + 1)
+        return pltpu.make_async_remote_copy(
+            src_ref=held.at[chunk, lane, pl.ds(leaving(lane, stage), half)],
+            dst_ref=landed.at[chunk, lane, pl.ds(landing(stage), half)],
+            send_sem=stage_send.at[chunk, lane, stage],
+            recv_sem=stage_recv.at[chunk, lane, stage],
+            device_id=partner(orders[lane][stage]),
+            device_id_type=pl.DeviceIdType.MESH,
+        )
+
+    def last_copy(chunk, lane, step):
+        return pltpu.make_async_remote_copy(
+            src_ref=held.at[chunk, lane, base(lane, levels), (head + step) % head_size],
+            dst_ref=last.at[chunk, lane, step - 1],
+            send_sem=last_send.at[chunk, lane, step - 1],
+            recv_sem=last_recv.at[chunk, lane, step - 1],
+            device_id=along(step),
+            device_id_type=pl.DeviceIdType.MESH,
+        )
+
+    def gathered(chunk, lane, stage, where, col):
+        total = held[chunk, lane, where, col].astype(f32) + got[chunk, lane, where, col].astype(f32)
+        for step in range(stage):
+            total = total + landed[chunk, lane, landing(step) + where - base(lane, step + 1), col].astype(f32)
+        return total
+
+    def send_on(chunk, lane, stage):
+        if stage == 0:
+            if lane == 0:
+                core_copy(chunk).wait()
+        else:
+            stage_copy(chunk, lane, stage - 1).wait()
+        if stage < levels:
+            half = outer >> (stage + 1)
+            start = leaving(lane, stage)
+
+            def add(step, carry):
+                where, col = start + step // head_size, step % head_size
+                held[chunk, lane, where, col] = gathered(chunk, lane, stage, where, col).astype(bf16)
+                return carry
+
+            lax.fori_loop(0, half * head_size, add, 0)
+            stage_copy(chunk, lane, stage).start()
+            return
+        where = base(lane, levels)
+        for step in range(1, head_size):
+            col = (head + step) % head_size
+            held[chunk, lane, where, col] = gathered(chunk, lane, stage, where, col).astype(bf16)
+            last_copy(chunk, lane, step).start()
+
     def advance(chunk, stage):
-        copy(chunk, stage).wait()
-        half = tiles >> (stage + 1)
-        keep = base(chunk, stage + 1)
-        if stage == stages - 1:
-            total = held[chunk, keep].astype(f32) + landed[chunk, landing(stage)].astype(f32)
+        for lane in range(2):
+            send_on(chunk, lane, stage)
+
+    def finish(chunk):
+        for lane in range(2):
+            total = gathered(chunk, lane, levels, base(lane, levels), head)
+            for step in range(1, head_size):
+                last_copy(chunk, lane, step).wait()
+                total = total + last[chunk, lane, step - 1].astype(f32)
+            rows = slice(lane * part_rows, (lane + 1) * part_rows)
             if chunk == 0:
-                grad_out[...] = total
+                grad_out[rows, :] = total
             else:
-                grad_qkv[chunk - 1] = total
-            return
-
-        def add(step, carry):
-            total = held[chunk, keep + step].astype(f32) + landed[chunk, landing(stage) + step].astype(f32)
-            held[chunk, keep + step] = total.astype(bf16)
+                grad_qkv[chunk - 1, rows, :] = total
+
+    def products(chunk, target, parity, left, right, depth):
+        def one(col, carry):
+            cols = pl.ds(pl.multiple_of(col * tile_cols, tile_cols), tile_cols)
+            product = dot(left[parity, :, depth], right[:, cols], ((1,), (0,))).astype(bf16)
+            for block in range(outer):
+                for lane in range(2):
+                    start = block * tile_rows + lane * part_rows
+                    target[chunk, lane, spot(lane, block), col] = product[start : start + part_rows]
             return carry
 
-        lax.fori_loop(0, half, add, 0)
-        copy(chunk, stage + 1).start()
-
-    def tile_place(chunk, axis, index):
-        total = 0
-        for step, (name, bit) in enumerate(orders[chunk]):
-            if name == axis:
-                total = total + ((index // 2**bit) % 2) * (tiles >> (step + 1))
-        return total
-
-    def products(chunk, left, right, depth, half):
-        def one(step, carry):
-            block = 2 * step + half
-            rows = pl.ds(pl.multiple_of(block * tile_rows, tile_rows), tile_rows)
-            product = dot(left[rows, depth], right[...], ((1,), (0,))).astype(bf16)
-            down = tile_place(chunk, "seq", block)
-            for col in range(head_size):
-                held[chunk, down + tile_place(chunk, "head", col)] = product[
-                    :, col * tile_cols : (col + 1) * tile_cols
-                ]
-            return carry
-
-        lax.fori_loop(0, seq_size // 2, one, 0)
+        lax.fori_loop(0, head_size, one, 0)
 
     def launch(chunk, left, right, depth):
-        mine = bit_at(orders[chunk][0])
-        products(chunk, left, right, depth, 1 - mine)
-        copy(chunk, 0).start()
-        products(chunk, left, right, depth, mine)
-
-    lax.fori_loop(0, pairs, forward, 0)
-    launch(0, attended_t, cotangent, everything)
-    lax.fori_loop(0, pairs // 2, backward, 0)
-    advance(0, 0)
-    lax.fori_loop(pairs // 2, pairs, backward, 0)
-    launch(1, normed_t, grad_query, own)
-    turn(0, WINDOW)
-    turn(WINDOW + length, 2 * WINDOW + length)
-    launch(2, normed_t, grad_pair.at[0], slice(0, 2 * WINDOW + length))
-    advance(1, 0)
-    launch(3, normed_t, grad_pair.at[1], slice(0, 2 * WINDOW + length))
-    advance(2, 0)
+        products(chunk, mail, 1 - core, left, right, depth)
+        core_copy(chunk).start()
+        products(chunk, held, core, left, right, depth)
 
     def pair_back(rows, cols):
         term = dot(grad_pair[0, rows, :], w_qkv[1, cols, :], ((1,), (1,)))
         return term + dot(grad_pair[1, rows, :], w_qkv[2, cols, :], ((1,), (1,)))
 
+    def norm_back(step, carry):
+        rows = pl.ds(pl.multiple_of(step * few, few), few)
+        unit, inverse = standardise(frames[rows, :].astype(f32))
+        grad = grad_normed[rows, :].astype(bf16).astype(f32) * gain[...]
+        average = jnp.mean(grad, axis=-1, keepdims=True)
+        along_unit = jnp.mean(grad * unit, axis=-1, keepdims=True)
+        grad = inverse * (grad - average - unit * along_unit)
+        grad_frames[rows, :] = (cotangent[rows, :].astype(f32) + grad).astype(bf16)
+        return carry
+
+    whole = slice(0, 2 * WINDOW + length)
+    lax.fori_loop(0, pairs, forward, 0)
+    launch(0, attended_t, cotangent, everything)
+    lax.fori_loop(0, 1, backward, 0)
+    advance(0, 0)
+    lax.fori_loop(1, pairs, backward, 0)
+    turn(0, WINDOW)
+    turn(WINDOW + length, 2 * WINDOW + length)
+    launch(3, normed_t, grad_pair.at[1], whole)
+    advance(0, 1)
+    advance(3, 0)
+    launch(2, normed_t, grad_pair.at[0], whole)
+    advance(0, 2)
+    advance(2, 0)
+    launch(1, normed_t, grad_query, own)
+    advance(1, 0)
+    advance(3, 1)
     for side in range(2):
         start = side * (length + WINDOW)
         for strip_start in range(0, channels, strip):
             cols = slice(strip_start, strip_start + strip)
             edge_out[side, :, cols] = pair_back(slice(start, start + WINDOW), cols).astype(bf16)
         edge_copy(side).start()
-    advance(3, 0)
+    advance(3, 2)
     for start in range(0, channels, strip):
         cols = slice(start, start + strip)
         mixed = dot(attended[...], w_out[:, cols], ((1,), (0,)))
         output[:, cols] = (frames[:, cols].astype(f32) + mixed).astype(bf16)
-    advance(0, 1)
+    advance(2, 1)
     for start in range(0, channels, strip):
         cols = slice(start, start + strip)
         grad_normed[:, cols] = pair_back(own, cols) + dot(grad_query[...], w_qkv[0, cols, :], ((1,), (1,)))
     advance(1, 1)
-    advance(2, 1)
-    advance(3, 1)
-
-    def norm_back(step, carry):
-        rows = pl.ds(pl.multiple_of(step * few, few), few)
-        unit, inverse = standardise(frames[rows, :].astype(f32))
-        grad = grad_normed[rows, :].astype(bf16).astype(f32) * gain[...]
-        average = jnp.mean(grad, axis=-1, keepdims=True)
-        along = jnp.mean(grad * unit, axis=-1, keepdims=True)
-        grad = inverse * (grad - average - unit * along)
-        grad_frames[rows, :] = (cotangent[rows, :].astype(f32) + grad).astype(bf16)
-        return carry
-
-    for stage in range(2, stages):
-        for chunk in range(chunks):
-            advance(chunk, stage)
-        if stage == 2:
-            edge_copy(0).wait()
-            edge_copy(1).wait()
-            grad_normed[:WINDOW, :] += edge_in[1].astype(f32)
-            grad_normed[length - WINDOW :, :] += edge_in[0].astype(f32)
-            lax.fori_loop(0, length // few, norm_back, 0)
+    advance(2, 2)
+    finish(0)
+    edge_copy(0).wait()
+    edge_copy(1).wait()
+    grad_normed[:WINDOW, :] += edge_in[1].astype(f32)
+    grad_normed[length - WINDOW :, :] += edge_in[0].astype(f32)
+    lax.fori_loop(0, length // few, norm_back, 0)
+    advance(1, 2)
+    finish(3)
+    finish(2)
+    finish(1)
 
 
 def deliver_kernel(scale, output, grad_frames, grad_qkv, grad_out, *targets):
@@ -339,16 +397,9 @@
     devices = seq_size * head_size
     bordered = length + 2 * WINDOW
     tile_rows, tile_cols = channels // seq_size, channels // head_size
-    outer = [("seq", bit) for bit in bits_of(seq_size)[1:]]
-    along = [("head", bit) for bit in bits_of(head_size)]
-    first = [("seq", 0)]
-    orders = [
-        first + outer + along,
-        first + outer[::-1] + along,
-        first + along[:1] + outer[::-1] + along[1:],
-        first + outer[:1] + along[:1] + outer[1:] + along[1:],
-    ]
-    chunks, stages = len(orders), len(orders[0])
+    chunks, outer = 4, seq_size // 2
+    levels = len(bits_of(outer))
+    part = (tile_rows // 2, tile_cols)
     bf16, f32 = jnp.bfloat16, jnp.float32
     vmem, anywhere = pl.BlockSpec(memory_space=pltpu.VMEM), pl.BlockSpec(memory_space=pl.ANY)
     dma = pltpu.SemaphoreType.DMA
@@ -359,7 +410,7 @@
         jax.ShapeDtypeStruct((tile_rows, tile_cols), f32),
     ]
     results = pl.pallas_call(
-        functools.partial(block_kernel, (seq_size, head_size), orders),
+        functools.partial(block_kernel, (seq_size, head_size)),
         out_shape=shapes,
         in_specs=[vmem, vmem, vmem, anywhere, anywhere],
         out_specs=[vmem] * 4,
@@ -367,29 +418,36 @@
             pltpu.VMEM((3, channels, channels), bf16),
             pltpu.VMEM((channels, channels), bf16),
             pltpu.VMEM((bordered, channels), bf16),
-            pltpu.VMEM((channels, bordered), bf16),
+            pltpu.VMEM((2, channels // 2, bordered), bf16),
             pltpu.VMEM((length, channels), bf16),
             pltpu.VMEM((bordered, channels), bf16),
             pltpu.VMEM((bordered, channels), bf16),
             pltpu.VMEM((length, channels), bf16),
             pltpu.VMEM((length, channels), bf16),
-            pltpu.VMEM((channels, length), bf16),
+            pltpu.VMEM((2, channels // 2, length), bf16),
             pltpu.VMEM((length, channels), bf16),
             pltpu.VMEM((2, bordered, channels), bf16),
             pltpu.VMEM((channels // HEAD_SIZE, length // WINDOW, WINDOW, 3 * WINDOW), bf16),
             pltpu.VMEM((2, WINDOW, channels), bf16),
             pltpu.VMEM((2, WINDOW, channels), bf16),
             pltpu.VMEM((length, channels), f32),
-            pltpu.VMEM((chunks, devices, tile_rows, tile_cols), bf16),
-            pltpu.VMEM((chunks, devices, tile_rows, tile_cols), bf16),
             pltpu.VMEM((2, WINDOW, channels), bf16),
+            pltpu.VMEM((chunks, 2, outer, head_size, *part), bf16),
+            pltpu.VMEM((chunks, 2, outer, head_size, *part), bf16),
+            pltpu.VMEM((chunks, 2, outer, head_size, *part), bf16),
+            pltpu.VMEM((chunks, 2, outer - 1, head_size, *part), bf16),
+            pltpu.VMEM((chunks, 2, head_size - 1, *part), bf16),
             dma((4,)),
             dma((2,)),
             dma((2,)),
             dma((2,)),
             dma((2,)),
-            dma((chunks, stages)),
-            dma((chunks, stages)),
+            dma((chunks,)),
+            dma((chunks,)),
+            dma((chunks, 2, levels)),
+            dma((chunks, 2, levels)),
+            dma((chunks, 2, head_size - 1)),
+            dma((chunks, 2, head_size - 1)),
         ],
         compiler_params=pltpu.CompilerParams(
             collective_id=0, has_side_effects=True, vmem_limit_bytes=60 * 2**20

time: 95.9 us -> 88.4 us (0.922)
  Pallas kernels: 95.1 us -> 87.6 us
    pallas_call x1, Pallas kernels: 92.6 us -> 85.1 us  [shards(): pl.pallas_call(functools.partial(block_kernel, (seq_size, head_size)), ou...]
where the time goes in v1:
time: 88.4 us; the launch traced here: 88.3 us
  Pallas kernels  87.6 us (99%)
    pallas_call x1, Pallas kernels, shards(): pl.pallas_call(functools.partial(block_kernel, (seq_size, head_size)), ou...  85.1 us
    pallas_call x1, Pallas kernels, shards(): pl.pallas_call(functools.partial(deliver_kernel, (devices * length) ** (-...  2.51 us

profile of v1, /device:TPU:0, one launch (start us, length us, event | category | flops | bytes accessed | tf_op | source)
XLA Modules:
  0.0 88.3 jit_solution(9754760064683109931)
XLA Ops:
  0.6 85.1 %block.1 = (bf16[256,1024]{1,0:T(8,128)(2,1)}, bf16[256,1024]{1,0:T(8,128)(2,1)}, f32[3,128,256]{2,1,0:T(8,128)}, f32[128,256]{1,0:T(8,128)}) custom-call(bf16[256,1024]{1,0:T(8,128)(2,1)} %frames.1, bf16[256,1024]{1,0:T(8,128)(2,1)} %cotangent.1, f32[1,1024]{1,0:T(1,128)} %bitcast.1, bf16[3,1024,1024]{2,1,0:T(8,128)(2,1)} %w_qkv_hbm.1, ...), custom_call_target="tpu_custom_call" | custom-call | tf_op jit(solution)/shard_map/block/pallas_call | solution.py:412
  85.8 2.5 %deliver.1 = (bf16[256,1024]{1,0:T(8,128)(2,1)}, bf16[256,1024]{1,0:T(8,128)(2,1)}, f32[3,128,256]{2,1,0:T(8,128)}, f32[128,256]{1,0:T(8,128)}) custom-call(bf16[256,1024]{1,0:T(8,128)(2,1)} %get-tuple-element.8.output, bf16[256,1024]{1,0:T(8,128)(2,1)} %get-tuple-element.9.grad_frames, f32[3,128,256]{2,1,0:T(8,128)} %get-tuple-element.10.grad_qkv, ...), custom_call_target="tpu_custom_call" | custom-call | tf_op jit(solution)/shard_map/deliver/pallas_call | solution.py:458

commit v2 on v1

v2 whole, which is shorter than its diff:
```python
import functools

import jax
import jax.numpy as jnp
from jax import lax
from jax.experimental import pallas as pl
from jax.experimental.pallas import tpu as pltpu
from jax.sharding import PartitionSpec as P

HEAD_SIZE = 128
WINDOW = 128

EPSILON = 1e-05
MASKED = -1e30
AXES = ("seq", "head")


def dot(a, b, contract):
    return lax.dot_general(a, b, (contract, ((), ())), preferred_element_type=jnp.float32)


def bits_of(size):
    return list(range(size.bit_length() - 1))


def block_kernel(
    sizes,
    frames, cotangent, gain, w_qkv_hbm, w_out_hbm,
    output, grad_frames, grad_qkv, grad_out,
    w_qkv, w_out, normed, normed_t, query, key, value, upstream, attended, attended_t,
    grad_query, grad_pair, edge_out, edge_in, grad_normed, halo, halo_normed,
    mail, got, held, landed, last, mail_out, got_out, held_out, landed_out, last_out,
    weight_sem, halo_send, halo_recv, edge_send, edge_recv,
    core_send, core_recv, stage_send, stage_recv, last_send, last_recv, last_send_out, last_recv_out,
):
    seq_size, head_size = sizes
    devices = seq_size * head_size
    length, channels = frames.shape
    outer, part_rows, tile_cols = held_out.shape[1], held_out.shape[3], held_out.shape[4]
    tile_rows = 2 * part_rows
    bits = bits_of(outer)
    orders = (bits, bits[::-1])
    levels = len(bits)
    seq, head = lax.axis_index("seq"), lax.axis_index("head")
    core, row_block = seq % 2, seq // 2
    position = seq * head_size + head
    bf16, f32 = jnp.bfloat16, jnp.float32
    strip = min(256, channels)

    def neighbour(step):
        there = (position + step + devices) % devices
        return (there // head_size, there % head_size)

    def bit_at(bit):
        return (row_block // 2**bit) % 2

    def partner(bit):
        return (2 * (row_block + (1 - 2 * bit_at(bit)) * 2**bit) + core, head)

    def along(step):
        return (seq, (head + step) % head_size)

    wide = 2 * HEAD_SIZE
    pairs = channels // wide
    heads_each = tile_cols // HEAD_SIZE

    for slot in range(2 * pairs):
        real = slot // 2 + (slot % 2) * pairs
        there, here = pl.ds(real * HEAD_SIZE, HEAD_SIZE), pl.ds(slot * HEAD_SIZE, HEAD_SIZE)
        pltpu.make_async_copy(w_out_hbm.at[there], w_out.at[here], weight_sem.at[3]).start()
    for which in range(3):
        for slot in range(2 * pairs):
            real = slot // 2 + (slot % 2) * pairs
            there, here = pl.ds(real * HEAD_SIZE, HEAD_SIZE), pl.ds(slot * HEAD_SIZE, HEAD_SIZE)
            pltpu.make_async_copy(
                w_qkv_hbm.at[which, :, there], w_qkv.at[which, :, here], weight_sem.at[which]
            ).start()

    def weight_wait(which):
        if which == 3:
            pltpu.make_async_copy(w_out_hbm, w_out, weight_sem.at[3]).wait()
        else:
            pltpu.make_async_copy(w_qkv_hbm.at[which], w_qkv.at[which], weight_sem.at[which]).wait()

    other_core = (2 * row_block + 1 - core, head)
    greeted = [other_core] + [partner(bit) for bit in bits]
    greeted += [along(step) for step in range(1, head_size)] + [neighbour(1), neighbour(-1)]
    barrier = pltpu.get_barrier_semaphore()
    for device in greeted:
        pl.semaphore_signal(barrier, inc=1, device_id=device, device_id_type=pl.DeviceIdType.MESH)
    pl.semaphore_wait(barrier, len(greeted))

    def halo_copy(side):
        rows = pl.ds(length - WINDOW, WINDOW) if side == 0 else pl.ds(0, WINDOW)
        return pltpu.make_async_remote_copy(
            src_ref=frames.at[rows],
            dst_ref=halo.at[side],
            send_sem=halo_send.at[side],
            recv_sem=halo_recv.at[side],
            device_id=neighbour(1 if side == 0 else -1),
            device_id_type=pl.DeviceIdType.MESH,
        )

    halo_copy(0).start()
    halo_copy(1).start()

    def standardise(values):
        average = jnp.mean(values, axis=-1, keepdims=True)
        centered = values - average
        variance = jnp.mean(centered * centered, axis=-1, keepdims=True)
        inverse = lax.rsqrt(variance + EPSILON)
        return centered * inverse, inverse

    few = 64

    def norm_rows(source, target, target_row, rows):
        def one(step, carry):
            values = source[pl.ds(pl.multiple_of(step * few, few), few), :].astype(f32)
            rounded = (standardise(values)[0] * gain[...]).astype(bf16)
            target[pl.ds(pl.multiple_of(target_row + step * few, few), few), :] = rounded
            return carry

        lax.fori_loop(0, rows // few, one, 0)

    def multiply_into(target, rows, left, weight, side):
        for start in range(0, channels, strip):
            cols = slice(start, start + strip)
            other = weight[:, cols] if side == 0 else weight[cols, :]
            target[rows, cols] = dot(left, other, ((1,), (side,))).astype(target.dtype)

    norm_rows(frames, normed, 0, length)
    own = slice(WINDOW, WINDOW + length)

    piece = min(128, tile_rows)

    def store_turned(target, first, cols, turned):
        for start in range(0, 128, piece):
            block = (first + start) // tile_rows
            down = (block // 2) * tile_rows + (first + start) % tile_rows
            target[block % 2, pl.ds(pl.multiple_of(down, piece), piece), cols] = turned[start : start + piece]

    def turn(source, row, place, rows):
        for start in range(0, rows, 128):
            for col in range(0, channels, 128):
                tile = source[row + start : row + start + 128, col : col + 128]
                cols = slice(place + start, place + start + 128)
                store_turned(normed_t, col, cols, tile.astype(f32).T.astype(bf16))

    turn(normed, 0, WINDOW, length)
    weight_wait(3)
    everything = slice(0, length)
    multiply_into(upstream, everything, cotangent[...], w_out, 1)
    for which, target, rows in ((0, query, everything), (1, key, own), (2, value, own)):
        weight_wait(which)
        multiply_into(target, rows, normed[...], w_qkv.at[which], 0)
    for side in range(2):
        halo_copy(side).wait()
        norm_rows(halo.at[side], halo_normed, side * WINDOW, WINDOW)
    for which, target in ((1, key), (2, value)):
        for start in range(0, channels, strip):
            cols = slice(start, start + strip)
            both = dot(halo_normed[...], w_qkv[which, :, cols], ((1,), (0,))).astype(bf16)
            target[:WINDOW, cols] = both[:WINDOW]
            target[WINDOW + length :, cols] = both[WINDOW:]
    turn(halo_normed, 0, 0, WINDOW)
    turn(halo_normed, WINDOW, WINDOW + length, WINDOW)

    def edge_copy(side):
        return pltpu.make_async_remote_copy(
            src_ref=edge_out.at[side],
            dst_ref=edge_in.at[side],
            send_sem=edge_send.at[side],
            recv_sem=edge_recv.at[side],
            device_id=neighbour(-1 if side == 0 else 1),
            device_id_type=pl.DeviceIdType.MESH,
        )

    blocks = length // WINDOW
    span = 3 * WINDOW
    score_scale = HEAD_SIZE ** (-0.5)
    row = lax.broadcasted_iota(jnp.int32, (WINDOW, span), 0)
    col = lax.broadcasted_iota(jnp.int32, (WINDOW, span), 1)
    near = (col >= row) & (col <= row + 2 * WINDOW)

    def attend(pair):
        for member in range(2):
            lane = pl.multiple_of(pair * wide + member * HEAD_SIZE, HEAD_SIZE)
            lanes = pl.ds(lane, HEAD_SIZE)
            real = (pair + member * pairs) * HEAD_SIZE
            key_grads = [None] * (blocks + 2)
            value_grads = [None] * (blocks + 2)
            for block in range(blocks):
                rows = slice(block * WINDOW, (block + 1) * WINDOW)
                keys = slice(block * WINDOW, block * WINDOW + span)
                q, k, v, up = query[rows, lanes], key[keys, lanes], value[keys, lanes], upstream[rows, lanes]
                frame = position * length + (block - 1) * WINDOW + col
                allowed = near & (frame >= 0) & (frame < devices * length)
                scores = jnp.where(allowed, dot(q, k, ((1,), (1,))) * score_scale, MASKED)
                share = jnp.exp(scores - jnp.max(scores, axis=-1, keepdims=True))
                rounded = (share * (1.0 / jnp.sum(share, axis=-1, keepdims=True))).astype(bf16)
                mixed = dot(rounded, v, ((1,), (0,)))
                attended[rows, lanes] = mixed.astype(bf16)
                store_turned(attended_t, real, rows, mixed.T.astype(bf16))
                share = rounded.astype(f32)
                grad = dot(up, v, ((1,), (1,)))
                centre = jnp.sum(share * grad, axis=-1, keepdims=True)
                grad = (share * (grad - centre) * score_scale).astype(bf16)
                grad_query[rows, lanes] = dot(grad, k, ((1,), (0,))).astype(bf16)
                key_grad = dot(grad, q, ((0,), (0,)))
                value_grad = dot(rounded, up, ((0,), (0,)))
                for part in range(3):
                    piece = slice(part * WINDOW, (part + 1) * WINDOW)
                    for sums, term in ((key_grads, key_grad[piece]), (value_grads, value_grad[piece])):
                        before = sums[block + part]
                        sums[block + part] = term if before is None else before + term
            for which, sums in enumerate((key_grads, value_grads)):
                for block in range(blocks + 2):
                    rows = slice(block * WINDOW, (block + 1) * WINDOW)
                    grad_pair[which, rows, lanes] = sums[block].astype(bf16)

    def spot(lane, block):
        return sum(((block >> bit) & 1) * (outer >> (step + 1)) for step, bit in enumerate(orders[lane]))

    def base(lane, stage):
        total = 0
        for step in range(stage):
            total = total + bit_at(orders[lane][step]) * (outer >> (step + 1))
        return total

    def landing(stage):
        return outer - (outer >> stage)

    def leaving(lane, stage):
        return base(lane, stage) + (1 - bit_at(orders[lane][stage])) * (outer >> (stage + 1))

    def remote(source, target, send, recv, device):
        return pltpu.make_async_remote_copy(
            src_ref=source,
            dst_ref=target,
            send_sem=send,
            recv_sem=recv,
            device_id=device,
            device_id_type=pl.DeviceIdType.MESH,
        )

    def core_copy(mail, got, chunk):
        return remote(mail, got, core_send.at[chunk], core_recv.at[chunk], other_core)

    def stage_copy(held, landed, chunk, lane, stage):
        half = outer >> (stage + 1)
        return remote(
            held.at[lane, pl.ds(leaving(lane, stage), half)],
            landed.at[lane, pl.ds(landing(stage), half)],
            stage_send.at[chunk, lane, stage],
            stage_recv.at[chunk, lane, stage],
            partner(orders[lane][stage]),
        )

    def gathered(bufs, lane, stage, where, *index):
        held, got, landed = bufs
        total = held[lane, where, *index].astype(f32) + got[lane, where, *index].astype(f32)
        for step in range(stage):
            place = landing(step) + where - base(lane, step + 1)
            total = total + landed[lane, place, *index].astype(f32)
        return total

    def reduce_stage(bufs, chunk, lane, stage, inner):
        held, got, landed = bufs
        half = outer >> (stage + 1)
        start = leaving(lane, stage)

        def add(step, carry):
            where, index = start + step // inner, step % inner
            held[lane, where, index] = gathered(bufs, lane, stage, where, index).astype(bf16)
            return carry

        lax.fori_loop(0, half * inner, add, 0)
        stage_copy(held, landed, chunk, lane, stage).start()

    def wait_stage(bufs, mail, chunk, lane, stage):
        held, got, landed = bufs
        if stage == 0:
            if lane == 0:
                core_copy(mail, got, chunk).wait()
        else:
            stage_copy(held, landed, chunk, lane, stage - 1).wait()

    def owner(pair, member):
        return (pair + member * pairs) // heads_each

    def tile_copy(pair, lane, member, away):
        return remote(
            held.at[pair, lane, base(lane, levels), member],
            last.at[pair, lane, member, away - 1],
            last_send.at[pair, lane, member],
            last_recv.at[pair, lane, member, away - 1],
            (seq, owner(pair, member)),
        )

    def advance(pair, stage):
        bufs = held.at[pair], got.at[pair], landed.at[pair]
        for lane in range(2):
            wait_stage(bufs, mail.at[pair], pair, lane, stage)
            if stage < levels:
                reduce_stage(bufs, pair, lane, stage, 2)
                continue
            where = base(lane, levels)
            for member in range(2):
                held[pair, lane, where, member] = gathered(bufs, lane, stage, where, member).astype(bf16)

                @pl.when(owner(pair, member) != head)
                def _():
                    tile_copy(pair, lane, member, (head - owner(pair, member) + head_size) % head_size).start()

    def finish(pair):
        for member in range(2):
            mine = owner(pair, member) == head
            inside = ((pair + member * pairs) % heads_each) * HEAD_SIZE

            @pl.when(mine)
            def _():
                for lane in range(2):
                    total = held[pair, lane, base(lane, levels), member].astype(f32)
                    for away in range(1, head_size):
                        tile_copy(pair, lane, member, away).wait_recv()
                        total = total + last[pair, lane, member, away - 1].astype(f32)
                    rows = slice(lane * part_rows, (lane + 1) * part_rows)
                    grad_qkv[:, rows, pl.ds(pl.multiple_of(inside, HEAD_SIZE), HEAD_SIZE)] = total

            @pl.when(jnp.logical_not(mine))
            def _():
                for lane in range(2):
                    tile_copy(pair, lane, member, 1).wait_send()

    def last_copy(lane, step):
        return remote(
            held_out.at[lane, base(lane, levels), (head + step) % head_size],
            last_out.at[lane, step - 1],
            last_send_out.at[lane, step - 1],
            last_recv_out.at[lane, step - 1],
            along(step),
        )

    def advance_out(stage):
        bufs = held_out, got_out, landed_out
        for lane in range(2):
            wait_stage(bufs, mail_out, pairs, lane, stage)
            if stage < levels:
                reduce_stage(bufs, pairs, lane, stage, head_size)
                continue
            where = base(lane, levels)
            for step in range(1, head_size):
                other = (head + step) % head_size
                held_out[lane, where, other] = gathered(bufs, lane, stage, where, other).astype(bf16)
                last_copy(lane, step).start()

    def finish_out():
        bufs = held_out, got_out, landed_out
        for lane in range(2):
            total = gathered(bufs, lane, levels, base(lane, levels), head)
            for step in range(1, head_size):
                last_copy(lane, step).wait()
                total = total + last_out[lane, step - 1].astype(f32)
            grad_out[lane * part_rows : (lane + 1) * part_rows, :] = total

    whole = slice(0, 2 * WINDOW + length)

    def products(pair, target, parity):
        cols = pl.ds(pl.multiple_of(pair * wide, wide), wide)
        for which in range(3):
            right = grad_query[:, cols] if which == 0 else grad_pair[which - 1, :, cols]
            product = dot(normed_t[parity, :, own if which == 0 else whole], right, ((1,), (0,))).astype(bf16)
            for block in range(outer):
                for lane in range(2):
                    start = block * tile_rows + lane * part_rows
                    for member in range(2):
                        target[pair, lane, spot(lane, block), member, which] = product[
                            start : start + part_rows, member * HEAD_SIZE : (member + 1) * HEAD_SIZE
                        ]

    def products_out(target, parity):
        def one(index, carry):
            cols = pl.ds(pl.multiple_of(index * tile_cols, tile_cols), tile_cols)
            product = dot(attended_t[parity], cotangent[:, cols], ((1,), (0,))).astype(bf16)
            for block in range(outer):
                for lane in range(2):
                    start = block * tile_rows + lane * part_rows
                    target[lane, spot(lane, block), index] = product[start : start + part_rows]
            return carry

        lax.fori_loop(0, head_size, one, 0)

    def pair_back(rows, cols):
        term = dot(grad_pair[0, rows, :], w_qkv[1, cols, :], ((1,), (1,)))
        return term + dot(grad_pair[1, rows, :], w_qkv[2, cols, :], ((1,), (1,)))

    def norm_back(step, carry):
        rows = pl.ds(pl.multiple_of(step * few, few), few)
        unit, inverse = standardise(frames[rows, :].astype(f32))
        grad = grad_normed[rows, :].astype(bf16).astype(f32) * gain[...]
        average = jnp.mean(grad, axis=-1, keepdims=True)
        along_unit = jnp.mean(grad * unit, axis=-1, keepdims=True)
        grad = inverse * (grad - average - unit * along_unit)
        grad_frames[rows, :] = (cotangent[rows, :].astype(f32) + grad).astype(bf16)
        return carry

    def pair_step(pair, carry):
        attend(pair)
        products(pair, mail, 1 - core)
        core_copy(mail.at[pair], got.at[pair], pair).start()
        products(pair, held, core)
        for stage in range(levels, -1, -1):

            @pl.when(pair >= stage)
            def _():
                advance(pair - stage, stage)

        return carry

    lax.fori_loop(0, pairs, pair_step, 0)

    def drain(step):
        for stage in range(levels, -1, -1):
            pair = pairs + step - stage
            if pair < pairs:
                advance(pair, stage)
            elif pair == pairs:
                advance_out(stage)

    products_out(mail_out, 1 - core)
    core_copy(mail_out, got_out, pairs).start()
    products_out(held_out, core)
    drain(0)
    for side in range(2):
        start = side * (length + WINDOW)
        for strip_start in range(0, channels, strip):
            cols = slice(strip_start, strip_start + strip)
            edge_out[side, :, cols] = pair_back(slice(start, start + WINDOW), cols).astype(bf16)
        edge_copy(side).start()
    drain(1)
    for start in range(0, channels, strip):
        cols = slice(start, start + strip)
        mixed = dot(attended[...], w_out[:, cols], ((1,), (0,)))
        output[:, cols] = (frames[:, cols].astype(f32) + mixed).astype(bf16)
    for start in range(0, channels, strip):
        cols = slice(start, start + strip)
        grad_normed[:, cols] = pair_back(own, cols) + dot(grad_query[...], w_qkv[0, cols, :], ((1,), (1,)))
    for step in range(2, levels + 1):
        drain(step)
    edge_copy(0).wait()
    edge_copy(1).wait()
    grad_normed[:WINDOW, :] += edge_in[1].astype(f32)
    grad_normed[length - WINDOW :, :] += edge_in[0].astype(f32)
    lax.fori_loop(0, length // few, norm_back, 0)

    def finish_pair(pair, carry):
        finish(pair)
        return carry

    lax.fori_loop(0, pairs, finish_pair, 0)
    finish_out()


def deliver_kernel(scale, output, grad_frames, grad_qkv, grad_out, *targets):
    targets[0][...] = output[...]
    targets[1][...] = grad_frames[...]
    targets[2][...] = grad_qkv[...] * scale
    targets[3][...] = grad_out[...] * scale


def shards(frames, cotangent, norm_gain, w_qkv, w_out):
    length, channels = frames.shape
    seq_size, head_size = lax.axis_size("seq"), lax.axis_size("head")
    devices = seq_size * head_size
    bordered = length + 2 * WINDOW
    tile_rows, tile_cols = channels // seq_size, channels // head_size
    outer, pairs = seq_size // 2, channels // (2 * HEAD_SIZE)
    levels = len(bits_of(outer))
    pair_part = (2, 3, tile_rows // 2, HEAD_SIZE)
    out_part = (tile_rows // 2, tile_cols)
    bf16, f32 = jnp.bfloat16, jnp.float32
    vmem, anywhere = pl.BlockSpec(memory_space=pltpu.VMEM), pl.BlockSpec(memory_space=pl.ANY)
    dma = pltpu.SemaphoreType.DMA
    shapes = [
        jax.ShapeDtypeStruct((length, channels), bf16),
        jax.ShapeDtypeStruct((length, channels), bf16),
        jax.ShapeDtypeStruct((3, tile_rows, tile_cols), f32),
        jax.ShapeDtypeStruct((tile_rows, tile_cols), f32),
    ]
    results = pl.pallas_call(
        functools.partial(block_kernel, (seq_size, head_size)),
        out_shape=shapes,
        in_specs=[vmem, vmem, vmem, anywhere, anywhere],
        out_specs=[vmem] * 4,
        scratch_shapes=[
            pltpu.VMEM((3, channels, channels), bf16),
            pltpu.VMEM((channels, channels), bf16),
            pltpu.VMEM((length, channels), bf16),
            pltpu.VMEM((2, channels // 2, bordered), bf16),
            pltpu.VMEM((length, channels), bf16),
            pltpu.VMEM((bordered, channels), bf16),
            pltpu.VMEM((bordered, channels), bf16),
            pltpu.VMEM((length, channels), bf16),
            pltpu.VMEM((length, channels), bf16),
            pltpu.VMEM((2, channels // 2, length), bf16),
            pltpu.VMEM((length, channels), bf16),
            pltpu.VMEM((2, bordered, channels), bf16),
            pltpu.VMEM((2, WINDOW, channels), bf16),
            pltpu.VMEM((2, WINDOW, channels), bf16),
            pltpu.VMEM((length, channels), f32),
            pltpu.VMEM((2, WINDOW, channels), bf16),
            pltpu.VMEM((2 * WINDOW, channels), bf16),
            pltpu.VMEM((pairs, 2, outer, *pair_part), bf16),
            pltpu.VMEM((pairs, 2, outer, *pair_part), bf16),
            pltpu.VMEM((pairs, 2, outer, *pair_part), bf16),
            pltpu.VMEM((pairs, 2, outer - 1, *pair_part), bf16),
            pltpu.VMEM((pairs, 2, 2, head_size - 1, *pair_part[1:]), bf16),
            pltpu.VMEM((2, outer, head_size, *out_part), bf16),
            pltpu.VMEM((2, outer, head_size, *out_part), bf16),
            pltpu.VMEM((2, outer, head_size, *out_part), bf16),
            pltpu.VMEM((2, outer - 1, head_size, *out_part), bf16),
            pltpu.VMEM((2, head_size - 1, *out_part), bf16),
            dma((4,)),
            dma((2,)),
            dma((2,)),
            dma((2,)),
            dma((2,)),
            dma((pairs + 1,)),
            dma((pairs + 1,)),
            dma((pairs + 1, 2, levels)),
            dma((pairs + 1, 2, levels)),
            dma((pairs, 2, 2)),
            dma((pairs, 2, 2, head_size - 1)),
            dma((2, head_size - 1)),
            dma((2, head_size - 1)),
        ],
        compiler_params=pltpu.CompilerParams(
            collective_id=0, has_side_effects=True, vmem_limit_bytes=60 * 2**20
        ),
        name="block",
    )(frames, cotangent, norm_gain.reshape(1, channels), w_qkv, w_out)
    return tuple(
        pl.pallas_call(
            functools.partial(deliver_kernel, (devices * length) ** (-0.5)),
            out_shape=shapes,
            in_specs=[vmem] * 4,
            out_specs=[vmem] * 4,
            name="deliver",
        )(*results)
    )


def solution(mesh):
    in_specs = (P(("seq", "head"), None), P(("seq", "head"), None), P(), P(), P())
    out_specs = (
        P(("seq", "head"), None),
        P(("seq", "head"), None),
        P(None, "seq", "head"),
        P("seq", "head"),
    )
    return jax.shard_map(shards, mesh=mesh, in_specs=in_specs, out_specs=out_specs, check_vma=False)
```

time: 88.4 us -> 84.7 us (0.958)
  Pallas kernels: 87.6 us -> 83.9 us
    pallas_call x1, Pallas kernels: 85.1 us -> 81.4 us  [shards(): pl.pallas_call(functools.partial(block_kernel, (seq_size, head_size)), ou...]
where the time goes in v2:
time: 84.7 us; the launch traced here: 84.6 us
  Pallas kernels  83.9 us (99%)
    pallas_call x1, Pallas kernels, shards(): pl.pallas_call(functools.partial(block_kernel, (seq_size, head_size)), ou...  81.4 us
    pallas_call x1, Pallas kernels, shards(): pl.pallas_call(functools.partial(deliver_kernel, (devices * length) ** (-...  2.51 us

profile of v2, /device:TPU:0, one launch (start us, length us, event | category | flops | bytes accessed | tf_op | source)
XLA Modules:
  0.0 84.6 jit_solution(5045878773854959775)
XLA Ops:
  0.6 81.4 %block.1 = (bf16[256,1024]{1,0:T(8,128)(2,1)}, bf16[256,1024]{1,0:T(8,128)(2,1)}, f32[3,128,256]{2,1,0:T(8,128)}, f32[128,256]{1,0:T(8,128)}) custom-call(bf16[256,1024]{1,0:T(8,128)(2,1)} %frames.1, bf16[256,1024]{1,0:T(8,128)(2,1)} %cotangent.1, f32[1,1024]{1,0:T(1,128)} %bitcast.1, bf16[3,1024,1024]{2,1,0:T(8,128)(2,1)} %w_qkv_hbm.1, ...), custom_call_target="tpu_custom_call" | custom-call | tf_op jit(solution)/shard_map/block/pallas_call | solution.py:490
  82.1 2.5 %deliver.1 = (bf16[256,1024]{1,0:T(8,128)(2,1)}, bf16[256,1024]{1,0:T(8,128)(2,1)}, f32[3,128,256]{2,1,0:T(8,128)}, f32[128,256]{1,0:T(8,128)}) custom-call(bf16[256,1024]{1,0:T(8,128)(2,1)} %get-tuple-element.8.output, bf16[256,1024]{1,0:T(8,128)(2,1)} %get-tuple-element.9.grad_frames, f32[3,128,256]{2,1,0:T(8,128)} %get-tuple-element.10.grad_qkv, ...), custom_call_target="tpu_custom_call" | custom-call | tf_op jit(solution)/shard_map/deliver/pallas_call | solution.py:543

commit v3 on v2

--- a/solution.py
+++ b/solution.py
@@ -25,17 +25,17 @@
 
 def block_kernel(
     sizes,
-    frames, cotangent, gain, w_qkv_hbm, w_out_hbm,
+    frames_hbm, cotangent_hbm, gain, w_qkv_hbm, w_out_hbm,
     output, grad_frames, grad_qkv, grad_out,
-    w_qkv, w_out, normed, normed_t, query, key, value, upstream, attended, attended_t,
-    grad_query, grad_pair, edge_out, edge_in, grad_normed, halo, halo_normed,
+    frames, cotangent, w_qkv, w_out, normed, normed_t, query, key, value, upstream, attended, attended_t,
+    grad_query, grad_pair, grad_sum, edge_out, edge_in, grad_normed, halo, halo_normed,
     mail, got, held, landed, last, mail_out, got_out, held_out, landed_out, last_out,
-    weight_sem, halo_send, halo_recv, edge_send, edge_recv,
+    rows_sem, weight_sem, halo_send, halo_recv, edge_send, edge_recv,
     core_send, core_recv, stage_send, stage_recv, last_send, last_recv, last_send_out, last_recv_out,
 ):
     seq_size, head_size = sizes
     devices = seq_size * head_size
-    length, channels = frames.shape
+    length, channels = frames_hbm.shape
     outer, part_rows, tile_cols = held_out.shape[1], held_out.shape[3], held_out.shape[4]
     tile_rows = 2 * part_rows
     bits = bits_of(outer)
@@ -63,6 +63,43 @@
     wide = 2 * HEAD_SIZE
     pairs = channels // wide
     heads_each = tile_cols // HEAD_SIZE
+
+    loads = [
+        pltpu.make_async_copy(frames_hbm, frames, rows_sem.at[0]),
+        pltpu.make_async_copy(cotangent_hbm, cotangent, rows_sem.at[1]),
+    ]
+    loads[0].start()
+
+    def weight_wait(which):
+        if which == 3:
+            pltpu.make_async_copy(w_out_hbm, w_out, weight_sem.at[3]).wait()
+        else:
+            pltpu.make_async_copy(w_qkv_hbm.at[which], w_qkv.at[which], weight_sem.at[which]).wait()
+
+    other_core = (2 * row_block + 1 - core, head)
+    greeted = [other_core] + [partner(bit) for bit in bits]
+    greeted += [along(step) for step in range(1, head_size)] + [neighbour(1), neighbour(-1)]
+    barrier = pltpu.get_barrier_semaphore()
+    for device in greeted:
+        pl.semaphore_signal(barrier, inc=1, device_id=device, device_id_type=pl.DeviceIdType.MESH)
+    pl.semaphore_wait(barrier, len(greeted))
+
+    def halo_copy(side):
+        rows = pl.ds(length - WINDOW, WINDOW) if side == 0 else pl.ds(0, WINDOW)
+        return pltpu.make_async_remote_copy(
+            src_ref=frames_hbm.at[rows],
+            dst_ref=halo.at[side],
+            send_sem=halo_send.at[side],
+            recv_sem=halo_recv.at[side],
+            device_id=neighbour(1 if side == 0 else -1),
+            device_id_type=pl.DeviceIdType.MESH,
+        )
+
+    at_start, at_end = head == 0, head == head_size - 1
+    pl.when(jnp.logical_not(at_end))(lambda: halo_copy(0).start())
+    pl.when(jnp.logical_not(at_start))(lambda: halo_copy(1).start())
+    near_side = (head == 0).astype(jnp.int32)
+    loads[1].start()
 
     for slot in range(2 * pairs):
         real = slot // 2 + (slot % 2) * pairs
@@ -76,33 +113,31 @@
                 w_qkv_hbm.at[which, :, there], w_qkv.at[which, :, here], weight_sem.at[which]
             ).start()
 
-    def weight_wait(which):
-        if which == 3:
-            pltpu.make_async_copy(w_out_hbm, w_out, weight_sem.at[3]).wait()
-        else:
-            pltpu.make_async_copy(w_qkv_hbm.at[which], w_qkv.at[which], weight_sem.at[which]).wait()
-
-    other_core = (2 * row_block + 1 - core, head)
-    greeted = [other_core] + [partner(bit) for bit in bits]
-    greeted += [along(step) for step in range(1, head_size)] + [neighbour(1), neighbour(-1)]
-    barrier = pltpu.get_barrier_semaphore()
-    for device in greeted:
-        pl.semaphore_signal(barrier, inc=1, device_id=device, device_id_type=pl.DeviceIdType.MESH)
-    pl.semaphore_wait(barrier, len(greeted))
-
-    def halo_copy(side):
-        rows = pl.ds(length - WINDOW, WINDOW) if side == 0 else pl.ds(0, WINDOW)
-        return pltpu.make_async_remote_copy(
-            src_ref=frames.at[rows],
+
+    def send_far():
+        @pl.when(at_end)
+        def _():
+            halo_copy(1).wait_send()
+            halo_copy(0).start()
+
+        @pl.when(at_start)
+        def _():
+            halo_copy(0).wait_send()
+            halo_copy(1).start()
+
+    def halo_wait(side):
+        pltpu.make_async_remote_copy(
+            src_ref=frames_hbm.at[pl.ds(0, WINDOW)],
             dst_ref=halo.at[side],
             send_sem=halo_send.at[side],
             recv_sem=halo_recv.at[side],
-            device_id=neighbour(1 if side == 0 else -1),
+            device_id=neighbour(1),
             device_id_type=pl.DeviceIdType.MESH,
-        )
-
-    halo_copy(0).start()
-    halo_copy(1).start()
+        ).wait_recv()
+
+    def halo_sent():
+        pl.when(jnp.logical_not(at_end))(lambda: halo_copy(1).wait_send())
+        pl.when(jnp.logical_not(at_start))(lambda: halo_copy(0).wait_send())
 
     def standardise(values):
         average = jnp.mean(values, axis=-1, keepdims=True)
@@ -128,6 +163,7 @@
             other = weight[:, cols] if side == 0 else weight[cols, :]
             target[rows, cols] = dot(left, other, ((1,), (side,))).astype(target.dtype)
 
+    loads[0].wait()
     norm_rows(frames, normed, 0, length)
     own = slice(WINDOW, WINDOW + length)
 
@@ -142,28 +178,34 @@
     def turn(source, row, place, rows):
         for start in range(0, rows, 128):
             for col in range(0, channels, 128):
-                tile = source[row + start : row + start + 128, col : col + 128]
-                cols = slice(place + start, place + start + 128)
+                down = pl.ds(pl.multiple_of(row + start, 128), 128)
+                cols = pl.ds(pl.multiple_of(place + start, 128), 128)
+                tile = source[down, col : col + 128]
                 store_turned(normed_t, col, cols, tile.astype(f32).T.astype(bf16))
 
     turn(normed, 0, WINDOW, length)
     weight_wait(3)
+    loads[1].wait()
     everything = slice(0, length)
     multiply_into(upstream, everything, cotangent[...], w_out, 1)
+    send_far()
     for which, target, rows in ((0, query, everything), (1, key, own), (2, value, own)):
         weight_wait(which)
         multiply_into(target, rows, normed[...], w_qkv.at[which], 0)
-    for side in range(2):
-        halo_copy(side).wait()
-        norm_rows(halo.at[side], halo_normed, side * WINDOW, WINDOW)
-    for which, target in ((1, key), (2, value)):
-        for start in range(0, channels, strip):
-            cols = slice(start, start + strip)
-            both = dot(halo_normed[...], w_qkv[which, :, cols], ((1,), (0,))).astype(bf16)
-            target[:WINDOW, cols] = both[:WINDOW]
-            target[WINDOW + length :, cols] = both[WINDOW:]
-    turn(halo_normed, 0, 0, WINDOW)
-    turn(halo_normed, WINDOW, WINDOW + length, WINDOW)
+
+    def halo_rows(side):
+        halo_wait(side)
+        first = pl.multiple_of(side * WINDOW, WINDOW)
+        start = pl.multiple_of(side * (length + WINDOW), WINDOW)
+        norm_rows(halo.at[side], halo_normed, first, WINDOW)
+        turn(halo_normed, first, start, WINDOW)
+
+    def halo_project(side, cols):
+        first = pl.multiple_of(side * WINDOW, WINDOW)
+        start = pl.multiple_of(side * (length + WINDOW), WINDOW)
+        for which, target in ((1, key), (2, value)):
+            made = dot(halo_normed[pl.ds(first, WINDOW), :], w_qkv[which, :, cols], ((1,), (0,)))
+            target[pl.ds(start, WINDOW), cols] = made.astype(bf16)
 
     def edge_copy(side):
         return pltpu.make_async_remote_copy(
@@ -182,41 +224,37 @@
     col = lax.broadcasted_iota(jnp.int32, (WINDOW, span), 1)
     near = (col >= row) & (col <= row + 2 * WINDOW)
 
-    def attend(pair):
+    def attend(pair, block):
         for member in range(2):
             lane = pl.multiple_of(pair * wide + member * HEAD_SIZE, HEAD_SIZE)
             lanes = pl.ds(lane, HEAD_SIZE)
             real = (pair + member * pairs) * HEAD_SIZE
-            key_grads = [None] * (blocks + 2)
-            value_grads = [None] * (blocks + 2)
-            for block in range(blocks):
-                rows = slice(block * WINDOW, (block + 1) * WINDOW)
-                keys = slice(block * WINDOW, block * WINDOW + span)
-                q, k, v, up = query[rows, lanes], key[keys, lanes], value[keys, lanes], upstream[rows, lanes]
-                frame = position * length + (block - 1) * WINDOW + col
-                allowed = near & (frame >= 0) & (frame < devices * length)
-                scores = jnp.where(allowed, dot(q, k, ((1,), (1,))) * score_scale, MASKED)
-                share = jnp.exp(scores - jnp.max(scores, axis=-1, keepdims=True))
-                rounded = (share * (1.0 / jnp.sum(share, axis=-1, keepdims=True))).astype(bf16)
-                mixed = dot(rounded, v, ((1,), (0,)))
-                attended[rows, lanes] = mixed.astype(bf16)
-                store_turned(attended_t, real, rows, mixed.T.astype(bf16))
-                share = rounded.astype(f32)
-                grad = dot(up, v, ((1,), (1,)))
-                centre = jnp.sum(share * grad, axis=-1, keepdims=True)
-                grad = (share * (grad - centre) * score_scale).astype(bf16)
-                grad_query[rows, lanes] = dot(grad, k, ((1,), (0,))).astype(bf16)
-                key_grad = dot(grad, q, ((0,), (0,)))
-                value_grad = dot(rounded, up, ((0,), (0,)))
-                for part in range(3):
-                    piece = slice(part * WINDOW, (part + 1) * WINDOW)
-                    for sums, term in ((key_grads, key_grad[piece]), (value_grads, value_grad[piece])):
-                        before = sums[block + part]
-                        sums[block + part] = term if before is None else before + term
-            for which, sums in enumerate((key_grads, value_grads)):
-                for block in range(blocks + 2):
-                    rows = slice(block * WINDOW, (block + 1) * WINDOW)
-                    grad_pair[which, rows, lanes] = sums[block].astype(bf16)
+            start = pl.multiple_of(block * WINDOW, WINDOW)
+            rows, keys = pl.ds(start, WINDOW), pl.ds(start, span)
+            q, k, v, up = query[rows, lanes], key[keys, lanes], value[keys, lanes], upstream[rows, lanes]
+            frame = position * length + (block - 1) * WINDOW + col
+            allowed = near & (frame >= 0) & (frame < devices * length)
+            scores = jnp.where(allowed, dot(q, k, ((1,), (1,))) * score_scale, MASKED)
+            share = jnp.exp(scores - jnp.max(scores, axis=-1, keepdims=True))
+            rounded = (share * (1.0 / jnp.sum(share, axis=-1, keepdims=True))).astype(bf16)
+            mixed = dot(rounded, v, ((1,), (0,)))
+            attended[rows, lanes] = mixed.astype(bf16)
+            store_turned(attended_t, real, rows, mixed.T.astype(bf16))
+            share = rounded.astype(f32)
+            grad = dot(up, v, ((1,), (1,)))
+            centre = jnp.sum(share * grad, axis=-1, keepdims=True)
+            grad = (share * (grad - centre) * score_scale).astype(bf16)
+            grad_query[rows, lanes] = dot(grad, k, ((1,), (0,))).astype(bf16)
+            grad_sum[0, keys, lanes] += dot(grad, q, ((0,), (0,)))
+            grad_sum[1, keys, lanes] += dot(rounded, up, ((0,), (0,)))
+
+    def near_step(pair, carry):
+        cols = pl.ds(pl.multiple_of(pair * wide, wide), wide)
+        grad_sum[:, :, cols] = jnp.zeros((2, length + 2 * WINDOW, wide), f32)
+        halo_project(near_side, cols)
+        for step in range(blocks - 1):
+            attend(pair, near_side + step)
+        return carry
 
     def spot(lane, block):
         return sum(((block >> bit) & 1) * (outer >> (step + 1)) for step, bit in enumerate(orders[lane]))
@@ -405,11 +443,19 @@
         return carry
 
     def pair_step(pair, carry):
-        attend(pair)
+        cols = pl.ds(pl.multiple_of(pair * wide, wide), wide)
+        halo_project(1 - near_side, cols)
+        attend(pair, (1 - near_side) * (blocks - 1))
+        grad_pair[:, :, cols] = grad_sum[:, :, cols].astype(bf16)
         products(pair, mail, 1 - core)
         core_copy(mail.at[pair], got.at[pair], pair).start()
         products(pair, held, core)
-        for stage in range(levels, -1, -1):
+
+        @pl.when(pair < pairs - 1)
+        def _():
+            near_step(pair + 1, 0)
+
+        for stage in range(levels + 1):
 
             @pl.when(pair >= stage)
             def _():
@@ -417,6 +463,10 @@
 
         return carry
 
+    halo_rows(near_side)
+    lax.fori_loop(0, 1, near_step, 0)
+    halo_rows(1 - near_side)
+    halo_sent()
     lax.fori_loop(0, pairs, pair_step, 0)
 
     def drain(step):
@@ -427,16 +477,16 @@
             elif pair == pairs:
                 advance_out(stage)
 
-    products_out(mail_out, 1 - core)
-    core_copy(mail_out, got_out, pairs).start()
-    products_out(held_out, core)
-    drain(0)
     for side in range(2):
         start = side * (length + WINDOW)
         for strip_start in range(0, channels, strip):
             cols = slice(strip_start, strip_start + strip)
             edge_out[side, :, cols] = pair_back(slice(start, start + WINDOW), cols).astype(bf16)
         edge_copy(side).start()
+    products_out(mail_out, 1 - core)
+    core_copy(mail_out, got_out, pairs).start()
+    products_out(held_out, core)
+    drain(0)
     drain(1)
     for start in range(0, channels, strip):
         cols = slice(start, start + strip)
@@ -490,9 +540,11 @@
     results = pl.pallas_call(
         functools.partial(block_kernel, (seq_size, head_size)),
         out_shape=shapes,
-        in_specs=[vmem, vmem, vmem, anywhere, anywhere],
+        in_specs=[anywhere, anywhere, vmem, anywhere, anywhere],
         out_specs=[vmem] * 4,
         scratch_shapes=[
+            pltpu.VMEM((length, channels), bf16),
+            pltpu.VMEM((length, channels), bf16),
             pltpu.VMEM((3, channels, channels), bf16),
             pltpu.VMEM((channels, channels), bf16),
             pltpu.VMEM((length, channels), bf16),
@@ -505,6 +557,7 @@
             pltpu.VMEM((2, channels // 2, length), bf16),
             pltpu.VMEM((length, channels), bf16),
             pltpu.VMEM((2, bordered, channels), bf16),
+            pltpu.VMEM((2, bordered, channels), f32),
             pltpu.VMEM((2, WINDOW, channels), bf16),
             pltpu.VMEM((2, WINDOW, channels), bf16),
             pltpu.VMEM((length, channels), f32),
@@ -520,6 +573,7 @@
             pltpu.VMEM((2, outer, head_size, *out_part), bf16),
             pltpu.VMEM((2, outer - 1, head_size, *out_part), bf16),
             pltpu.VMEM((2, head_size - 1, *out_part), bf16),
+            dma((2,)),
             dma((4,)),
             dma((2,)),
             dma((2,)),

time: 84.7 us -> 80.2 us (0.947)
  Pallas kernels: 83.9 us -> 79.4 us
    pallas_call x1, Pallas kernels: 81.4 us -> 76.9 us  [shards(): pl.pallas_call(functools.partial(block_kernel, (seq_size, head_size)), ou...]
where the time goes in v3:
time: 80.2 us; the launch traced here: 80.1 us
  Pallas kernels  79.4 us (99%)
    pallas_call x1, Pallas kernels, shards(): pl.pallas_call(functools.partial(block_kernel, (seq_size, head_size)), ou...  76.9 us
    pallas_call x1, Pallas kernels, shards(): pl.pallas_call(functools.partial(deliver_kernel, (devices * length) ** (-...  2.51 us

profile of v3, /device:TPU:0, one launch (start us, length us, event | category | flops | bytes accessed | tf_op | source)
XLA Modules:
  0.0 80.1 jit_solution(9948776331949407349)
XLA Ops:
  0.6 76.9 %block.1 = (bf16[256,1024]{1,0:T(8,128)(2,1)}, bf16[256,1024]{1,0:T(8,128)(2,1)}, f32[3,128,256]{2,1,0:T(8,128)}, f32[128,256]{1,0:T(8,128)}) custom-call(bf16[256,1024]{1,0:T(8,128)(2,1)} %frames_hbm.1, bf16[256,1024]{1,0:T(8,128)(2,1)} %cotangent_hbm.1, f32[1,1024]{1,0:T(1,128)} %bitcast.1, bf16[3,1024,1024]{2,1,0:T(8,128)(2,1)} %w_qkv_hbm.1, ...), custom_call_target="tpu_custom_call" | custom-call | tf_op jit(solution)/shard_map/block/pallas_call | solution.py:540
  77.5 2.5 %deliver.1 = (bf16[256,1024]{1,0:T(8,128)(2,1)}, bf16[256,1024]{1,0:T(8,128)(2,1)}, f32[3,128,256]{2,1,0:T(8,128)}, f32[128,256]{1,0:T(8,128)}) custom-call(bf16[256,1024]{1,0:T(8,128)(2,1)} %get-tuple-element.8.output, bf16[256,1024]{1,0:T(8,128)(2,1)} %get-tuple-element.9.grad_frames, f32[3,128,256]{2,1,0:T(8,128)} %get-tuple-element.10.grad_qkv, ...), custom_call_target="tpu_custom_call" | custom-call | tf_op jit(solution)/shard_map/deliver/pallas_call | solution.py:597

commit v4 on v3

--- a/solution.py
+++ b/solution.py
@@ -442,18 +442,32 @@
         grad_frames[rows, :] = (cotangent[rows, :].astype(f32) + grad).astype(bf16)
         return carry
 
-    def pair_step(pair, carry):
+    def send_edges():
+        for side in range(2):
+            start = side * (length + WINDOW)
+            for strip_start in range(0, channels, strip):
+                cols = slice(strip_start, strip_start + strip)
+                edge_out[side, :, cols] = pair_back(slice(start, start + WINDOW), cols).astype(bf16)
+            edge_copy(side).start()
+
+    def far_step(pair):
         cols = pl.ds(pl.multiple_of(pair * wide, wide), wide)
         halo_project(1 - near_side, cols)
         attend(pair, (1 - near_side) * (blocks - 1))
         grad_pair[:, :, cols] = grad_sum[:, :, cols].astype(bf16)
+
+    def pair_step(pair, carry):
         products(pair, mail, 1 - core)
         core_copy(mail.at[pair], got.at[pair], pair).start()
         products(pair, held, core)
 
         @pl.when(pair < pairs - 1)
         def _():
-            near_step(pair + 1, 0)
+            far_step(pair + 1)
+
+        @pl.when(pair == pairs - 1)
+        def _():
+            send_edges()
 
         for stage in range(levels + 1):
 
@@ -461,12 +475,17 @@
             def _():
                 advance(pair - stage, stage)
 
+        @pl.when(pair == 1)
+        def _():
+            near_step(pairs - 1, 0)
+
         return carry
 
     halo_rows(near_side)
-    lax.fori_loop(0, 1, near_step, 0)
+    lax.fori_loop(0, pairs - 1, near_step, 0)
     halo_rows(1 - near_side)
     halo_sent()
+    far_step(0)
     lax.fori_loop(0, pairs, pair_step, 0)
 
     def drain(step):
@@ -477,12 +496,6 @@
             elif pair == pairs:
                 advance_out(stage)
 
-    for side in range(2):
-        start = side * (length + WINDOW)
-        for strip_start in range(0, channels, strip):
-            cols = slice(strip_start, strip_start + strip)
-            edge_out[side, :, cols] = pair_back(slice(start, start + WINDOW), cols).astype(bf16)
-        edge_copy(side).start()
     products_out(mail_out, 1 - core)
     core_copy(mail_out, got_out, pairs).start()
     products_out(held_out, core)
@@ -539,7 +552,7 @@
     ]
     results = pl.pallas_call(
         functools.partial(block_kernel, (seq_size, head_size)),
-        out_shape=shapes,
+        out_shape=[pltpu.VMEM(one.shape, one.dtype) for one in shapes],
         in_specs=[anywhere, anywhere, vmem, anywhere, anywhere],
         out_specs=[vmem] * 4,
         scratch_shapes=[
@@ -600,7 +613,7 @@
             in_specs=[vmem] * 4,
             out_specs=[vmem] * 4,
             name="deliver",
-        )(*results)
+        )(*[pltpu.with_memory_space_constraint(one, pltpu.VMEM) for one in results])
     )
 
 

time: 80.2 us -> 77.5 us (0.966)
  Pallas kernels: 79.4 us -> 76.7 us
    pallas_call x1, Pallas kernels: 76.9 us -> 75.5 us  [shards(): pl.pallas_call(functools.partial(block_kernel, (seq_size, head_size)), ou...]
    pallas_call x1, Pallas kernels: 2.51 us -> 1.25 us  [shards(): pl.pallas_call(functools.partial(deliver_kernel, (devices * length) ** (-...]
where the time goes in v4:
time: 77.5 us; the launch traced here: 77.4 us
  Pallas kernels  76.7 us (99%)
    pallas_call x1, Pallas kernels, shards(): pl.pallas_call(functools.partial(block_kernel, (seq_size, head_size)), ou...  75.5 us

profile of v4, /device:TPU:0, one launch (start us, length us, event | category | flops | bytes accessed | tf_op | source)
XLA Modules:
  0.0 77.4 jit_solution(6095285112146547566)
XLA Ops:
  0.6 75.5 %block.1 = (bf16[256,1024]{1,0:T(8,128)(2,1)S(1)}, bf16[256,1024]{1,0:T(8,128)(2,1)S(1)}, f32[3,128,256]{2,1,0:T(8,128)S(1)}, f32[128,256]{1,0:T(8,128)S(1)}) custom-call(bf16[256,1024]{1,0:T(8,128)(2,1)} %frames_hbm.1, bf16[256,1024]{1,0:T(8,128)(2,1)} %cotangent_hbm.1, f32[1,1024]{1,0:T(1,128)} %bitcast.1, bf16[3,1024,1024]{2,1,0:T(8,128)(2,1)} %w_qkv_hbm.1, ...), custom_call_target="tpu_custom_call" | custom-call | tf_op jit(solution)/shard_map/block/pallas_call | solution.py:553
  76.1 1.2 %deliver.1 = (bf16[256,1024]{1,0:T(8,128)(2,1)}, bf16[256,1024]{1,0:T(8,128)(2,1)}, f32[3,128,256]{2,1,0:T(8,128)}, f32[128,256]{1,0:T(8,128)}) custom-call(bf16[256,1024]{1,0:T(8,128)(2,1)S(1)} %get-tuple-element.8.output, bf16[256,1024]{1,0:T(8,128)(2,1)S(1)} %get-tuple-element.9.grad_frames, f32[3,128,256]{2,1,0:T(8,128)S(1)} %get-tuple-element.10.grad_qkv, ...), custom_call_target="tpu_custom_call" | custom-call | tf_op jit(solution)/shard_map/deliver/pallas_call | solution.py:610

commit v5 on v4

--- a/solution.py
+++ b/solution.py
@@ -102,12 +102,12 @@
     loads[1].start()
 
     for slot in range(2 * pairs):
-        real = slot // 2 + (slot % 2) * pairs
+        real = (2 * pairs - 1 - slot // 2) if slot % 2 else slot // 2
         there, here = pl.ds(real * HEAD_SIZE, HEAD_SIZE), pl.ds(slot * HEAD_SIZE, HEAD_SIZE)
         pltpu.make_async_copy(w_out_hbm.at[there], w_out.at[here], weight_sem.at[3]).start()
     for which in range(3):
         for slot in range(2 * pairs):
-            real = slot // 2 + (slot % 2) * pairs
+            real = (2 * pairs - 1 - slot // 2) if slot % 2 else slot // 2
             there, here = pl.ds(real * HEAD_SIZE, HEAD_SIZE), pl.ds(slot * HEAD_SIZE, HEAD_SIZE)
             pltpu.make_async_copy(
                 w_qkv_hbm.at[which, :, there], w_qkv.at[which, :, here], weight_sem.at[which]
@@ -184,11 +184,11 @@
                 store_turned(normed_t, col, cols, tile.astype(f32).T.astype(bf16))
 
     turn(normed, 0, WINDOW, length)
+    send_far()
     weight_wait(3)
     loads[1].wait()
     everything = slice(0, length)
     multiply_into(upstream, everything, cotangent[...], w_out, 1)
-    send_far()
     for which, target, rows in ((0, query, everything), (1, key, own), (2, value, own)):
         weight_wait(which)
         multiply_into(target, rows, normed[...], w_qkv.at[which], 0)
@@ -224,11 +224,14 @@
     col = lax.broadcasted_iota(jnp.int32, (WINDOW, span), 1)
     near = (col >= row) & (col <= row + 2 * WINDOW)
 
+    def head_of(pair, member):
+        return 2 * pairs - 1 - pair if member else pair
+
     def attend(pair, block):
         for member in range(2):
             lane = pl.multiple_of(pair * wide + member * HEAD_SIZE, HEAD_SIZE)
             lanes = pl.ds(lane, HEAD_SIZE)
-            real = (pair + member * pairs) * HEAD_SIZE
+            real = head_of(pair, member) * HEAD_SIZE
             start = pl.multiple_of(block * WINDOW, WINDOW)
             rows, keys = pl.ds(start, WINDOW), pl.ds(start, span)
             q, k, v, up = query[rows, lanes], key[keys, lanes], value[keys, lanes], upstream[rows, lanes]
@@ -324,7 +327,7 @@
             stage_copy(held, landed, chunk, lane, stage - 1).wait()
 
     def owner(pair, member):
-        return (pair + member * pairs) // heads_each
+        return head_of(pair, member) // heads_each
 
     def tile_copy(pair, lane, member, away):
         return remote(
@@ -353,7 +356,7 @@
     def finish(pair):
         for member in range(2):
             mine = owner(pair, member) == head
-            inside = ((pair + member * pairs) % heads_each) * HEAD_SIZE
+            inside = (head_of(pair, member) % heads_each) * HEAD_SIZE
 
             @pl.when(mine)
             def _():
@@ -489,7 +492,7 @@
     lax.fori_loop(0, pairs, pair_step, 0)
 
     def drain(step):
-        for stage in range(levels, -1, -1):
+        for stage in range(levels + 1):
             pair = pairs + step - stage
             if pair < pairs:
                 advance(pair, stage)

time: 77.5 us -> 76.7 us (0.990)
  Pallas kernels: 76.7 us -> 75.8 us
    pallas_call x1, Pallas kernels: 75.5 us -> 74.6 us  [shards(): pl.pallas_call(functools.partial(block_kernel, (seq_size, head_size)), ou...]
where the time goes in v5:
time: 76.7 us; the launch traced here: 76.5 us
  Pallas kernels  75.8 us (99%)
    pallas_call x1, Pallas kernels, shards(): pl.pallas_call(functools.partial(block_kernel, (seq_size, head_size)), ou...  74.6 us

profile of v5, /device:TPU:0, one launch (start us, length us, event | category | flops | bytes accessed | tf_op | source)
XLA Modules:
  0.0 76.5 jit_solution(3242083860545398029)
XLA Ops:
  0.6 74.6 %block.1 = (bf16[256,1024]{1,0:T(8,128)(2,1)S(1)}, bf16[256,1024]{1,0:T(8,128)(2,1)S(1)}, f32[3,128,256]{2,1,0:T(8,128)S(1)}, f32[128,256]{1,0:T(8,128)S(1)}) custom-call(bf16[256,1024]{1,0:T(8,128)(2,1)} %frames_hbm.1, bf16[256,1024]{1,0:T(8,128)(2,1)} %cotangent_hbm.1, f32[1,1024]{1,0:T(1,128)} %bitcast.1, bf16[3,1024,1024]{2,1,0:T(8,128)(2,1)} %w_qkv_hbm.1, ...), custom_call_target="tpu_custom_call" | custom-call | tf_op jit(solution)/shard_map/block/pallas_call | solution.py:556
  75.2 1.2 %deliver.1 = (bf16[256,1024]{1,0:T(8,128)(2,1)}, bf16[256,1024]{1,0:T(8,128)(2,1)}, f32[3,128,256]{2,1,0:T(8,128)}, f32[128,256]{1,0:T(8,128)}) custom-call(bf16[256,1024]{1,0:T(8,128)(2,1)S(1)} %get-tuple-element.8.output, bf16[256,1024]{1,0:T(8,128)(2,1)S(1)} %get-tuple-element.9.grad_frames, f32[3,128,256]{2,1,0:T(8,128)S(1)} %get-tuple-element.10.grad_qkv, ...), custom_call_target="tpu_custom_call" | custom-call | tf_op jit(solution)/shard_map/deliver/pallas_call | solution.py:613

commit v6 on v5

--- a/solution.py
+++ b/solution.py
@@ -446,11 +446,17 @@
         return carry
 
     def send_edges():
+        def both(which):
+            return jnp.concatenate([grad_pair[which, :WINDOW, :], grad_pair[which, WINDOW + length :, :]], axis=0)
+
+        key_rows, value_rows = both(0), both(1)
+        for start in range(0, channels, strip):
+            cols = slice(start, start + strip)
+            made = dot(key_rows, w_qkv[1, cols, :], ((1,), (1,))) + dot(value_rows, w_qkv[2, cols, :], ((1,), (1,)))
+            made = made.astype(bf16)
+            edge_out[0, :, cols] = made[:WINDOW]
+            edge_out[1, :, cols] = made[WINDOW:]
         for side in range(2):
-            start = side * (length + WINDOW)
-            for strip_start in range(0, channels, strip):
-                cols = slice(strip_start, strip_start + strip)
-                edge_out[side, :, cols] = pair_back(slice(start, start + WINDOW), cols).astype(bf16)
             edge_copy(side).start()
 
     def far_step(pair):

time: 76.7 us -> 76.6 us (level)
  no operation moved by 1% of the time
where the time goes in v6:
time: 76.6 us; the launch traced here: 76.4 us
  Pallas kernels  75.8 us (99%)
    pallas_call x1, Pallas kernels, shards(): pl.pallas_call(functools.partial(block_kernel, (seq_size, head_size)), ou...  74.5 us

profile of v6, /device:TPU:0, one launch (start us, length us, event | category | flops | bytes accessed | tf_op | source)
XLA Modules:
  0.0 76.4 jit_solution(11702430525990455594)
XLA Ops:
  0.6 74.5 %block.1 = (bf16[256,1024]{1,0:T(8,128)(2,1)S(1)}, bf16[256,1024]{1,0:T(8,128)(2,1)S(1)}, f32[3,128,256]{2,1,0:T(8,128)S(1)}, f32[128,256]{1,0:T(8,128)S(1)}) custom-call(bf16[256,1024]{1,0:T(8,128)(2,1)} %frames_hbm.1, bf16[256,1024]{1,0:T(8,128)(2,1)} %cotangent_hbm.1, f32[1,1024]{1,0:T(1,128)} %bitcast.1, bf16[3,1024,1024]{2,1,0:T(8,128)(2,1)} %w_qkv_hbm.1, ...), custom_call_target="tpu_custom_call" | custom-call | tf_op jit(solution)/shard_map/block/pallas_call | solution.py:562
  75.1 1.2 %deliver.1 = (bf16[256,1024]{1,0:T(8,128)(2,1)}, bf16[256,1024]{1,0:T(8,128)(2,1)}, f32[3,128,256]{2,1,0:T(8,128)}, f32[128,256]{1,0:T(8,128)}) custom-call(bf16[256,1024]{1,0:T(8,128)(2,1)S(1)} %get-tuple-element.8.output, bf16[256,1024]{1,0:T(8,128)(2,1)S(1)} %get-tuple-element.9.grad_frames, f32[3,128,256]{2,1,0:T(8,128)S(1)} %get-tuple-element.10.grad_qkv, ...), custom_call_target="tpu_custom_call" | custom-call | tf_op jit(solution)/shard_map/deliver/pallas_call | solution.py:619
